TPU v7x, 32 devices: a whole 2x2x4 slice. The times are simulated.
32 devices in a mesh: seq: 8 (over z, y), head: 4 (over x, core).
Axes of the slice: x: 2, y: 2, z: 4, core: 2. Of those that a mesh axis runs over, the one named last changes fastest.
Arguments:
- inputs: bfloat16 [4, 4096, 768], P(None, 'seq'), may hold values from -6 to 6
- w_qkv: bfloat16 [3, 768, 768], P(None, None, 'head'), may hold values from -0.21875 to 0.21875
- b_qv: bfloat16 [2, 768], P(None, 'head'), may hold values from -4 to 4
- w_out: bfloat16 [768, 768], P('head'), may hold values from -1 to 1
- out_bias: bfloat16 [2, 768], replicated, may hold values from -4 to 4
- w_up: bfloat16 [768, 3072], P(None, 'head'), may hold values from -0.21875 to 0.21875
- b_up: bfloat16 [3072], P('head'), may hold values from -4 to 4
- w_down: bfloat16 [3072, 768], P('head'), may hold values from -0.109375 to 0.109375
- norm_gain: float32 [2, 768], replicated, may hold values from 0.5 to 1.5
- norm_shift: float32 [2, 768], replicated, may hold values from -3 to 3
- d_out: bfloat16 [4, 4096, 768], P(None, ('seq', 'head')), may hold values from -6 to 6
- q_perm: int32 [4, 12, 4096], P(None, 'head'), may hold values from 0 to 4095, as said below
- k_perm: int32 [4, 12, 4096], P(None, 'head'), may hold values from 0 to 4095, as said below
- masked: int32 [4, 1024], replicated, may hold values from 0 to 4095, as said below
Outputs:
- result: float32 [4, 4096, 768], P(None, ('seq', 'head'))
- d_inputs: float32 [4, 4096, 768], P(None, ('seq', 'head'))
- grad_qkv: float32 [3, 768, 768], P(None, 'seq', 'head')
- grad_bqv: float32 [2, 768], replicated
- grad_wout: float32 [768, 768], P('head', 'seq')
- grad_obias: float32 [2, 768], replicated
- grad_wup: float32 [768, 3072], P('seq', 'head')
- grad_bup: float32 [3072], replicated
- grad_wdown: float32 [3072, 768], P('head', 'seq')
- grad_gain: float32 [2, 768], replicated
- grad_shift: float32 [2, 768], replicated
- entropy: float32 [12, 128], P('head', 'seq')
- occupancy: int32 [12, 128], P('head', 'seq')
Inputs may be any that keep to these rules, and one draw needn't show every extreme that they name: `q_perm`: for each sequence and head a permutation of the 4096 positions. Cut the positions into aligned blocks of 512 and the slots into aligned runs of 2048: one block puts between 171 and 341 of its positions into one run, and 341 is reached for every sequence and head. `k_perm`: same law as q_perm, drawn independently. `masked`: each row lists 1024 distinct positions in increasing order.
All inputs are finite; a program needn't handle non-finite values.
Results may differ from a plain program's by a relative error of at most 0.015.
Values may be sent and summed in bfloat16 or wider, within the bound.
No kernel may reach another device: no remote copies, remote signals or barrier semaphores. Data moves between devices by JAX's collectives and lax.ppermute only.
A program may use at most 192 MiB of HBM per device.

v0:
```python
import functools

import jax
import jax.numpy as jnp
from jax import lax
from jax.experimental import pallas as pl
from jax.experimental.pallas import tpu as pltpu
from jax.sharding import Mesh
from jax.sharding import PartitionSpec as P

DH = 64
FF = 3072
CLUSTER = 128
LENGTH = 4096
TOK_DEV = 2048
OWN = LENGTH // TOK_DEV
EPS = 1e-06
PLANE = ("own", "hx", "hc")
HEAD = ("hx", "hc")
SEQ = ("sq", "own")
CHUNK = 512
STEPS = 3 * TOK_DEV // CHUNK
FULL_STEPS = 2 * TOK_DEV // CHUNK
GROUPS = CHUNK // CLUSTER
BF = jnp.bfloat16
F32 = jnp.float32
VMEM = 56 * 1024 * 1024
SIDE = 128


def cost(micros):
    return pl.CostEstimate(flops=micros * 10**9, transcendentals=0, bytes_accessed=micros * 10**6)


def nn(a, b):
    return lax.dot_general(a, b, (((1,), (0,)), ((), ())), preferred_element_type=F32)


def nt(a, b):
    return lax.dot_general(a, b, (((1,), (1,)), ((), ())), preferred_element_type=F32)


def tn(a, b):
    return lax.dot_general(a, b, (((0,), (0,)), ((), ())), preferred_element_type=F32)


def columns(count, body):
    def at(n, carry):
        body(pl.ds(pl.multiple_of(n * 256, 256), 256))
        return carry

    lax.fori_loop(0, count // 256, at, 0)


def clusters(body):
    def at(pair, carry):
        for j in range(2):
            c = 2 * pair + j
            body(c, pl.ds(pl.multiple_of(c * CLUSTER, CLUSTER), CLUSTER))
        return carry

    lax.fori_loop(0, GROUPS // 2, at, 0)


def log2(n):
    return n.bit_length() - 1


def prepare_body(
    block_len,
    heads,
    here_ref,
    q_ref,
    k_ref,
    slots_ref,
    masked_ref,
    pq_ref,
    pk_ref,
    pqr_ref,
    pkr_ref,
    mask_ref,
    listed_ref,
):
    share = block_len // heads

    def place(pos, size):
        block = pos >> log2(block_len)
        rest = pos & (block_len - 1)
        device = (block & (OWN - 1)) * heads + (rest >> log2(share))
        token = (block >> log2(OWN)) * share + (rest & (share - 1))
        return ((token >> log2(size)) << log2(size * OWN * heads)) + device * size + (token & (size - 1))

    for pos_ref, col_ref, row_ref, size in (
        (q_ref, pq_ref, pqr_ref, 128),
        (k_ref, pk_ref, pkr_ref, 256),
    ):

        def chunk(c, carry):
            row = place(pos_ref[c], size)
            row_ref[c] = row
            col_ref[c] = jnp.broadcast_to(row, (8, CHUNK)).T[:, :1]
            return carry

        lax.fori_loop(0, pos_ref.shape[0], chunk, 0)
    token = lax.broadcasted_iota(jnp.int32, mask_ref.shape, 0)
    own_pos = (
        (((token >> log2(share)) * OWN + here_ref[0]) << log2(block_len))
        + here_ref[1] * share
        + (token & (share - 1))
    )
    mask_ref[...] = jnp.max((own_pos == masked_ref[...]).astype(F32), 1, keepdims=True)
    masked_col = jnp.broadcast_to(masked_ref[...], (8, masked_ref.shape[1])).T[:, :1]

    def count(c, carry):
        listed_ref[c] = jnp.sum((slots_ref[c] == masked_col).astype(jnp.int32), 0, keepdims=True)
        return carry

    lax.fori_loop(0, slots_ref.shape[0], count, 0)


def prepare(block_len, heads, here, q_pos, k_pos, slots, masked_row, tokens):
    steps = q_pos.shape[0]
    vmem = pl.BlockSpec(memory_space=pltpu.VMEM)
    col = jax.ShapeDtypeStruct((steps, CHUNK, 1), jnp.int32)
    row = jax.ShapeDtypeStruct((steps, 1, CHUNK), jnp.int32)
    return pl.pallas_call(
        functools.partial(prepare_body, block_len, heads),
        in_specs=[pl.BlockSpec(memory_space=pltpu.SMEM), vmem, vmem, vmem, vmem],
        out_specs=[vmem] * 6,
        out_shape=[
            col,
            col,
            row,
            row,
            jax.ShapeDtypeStruct((tokens, 1), F32),
            jax.ShapeDtypeStruct(slots.shape, jnp.int32),
        ],
        compiler_params=pltpu.CompilerParams(vmem_limit_bytes=VMEM),
        name="prepare",
        cost_estimate=cost(1),
    )(here, q_pos, k_pos, slots, masked_row)


def plus(a, b):
    return (a.astype(F32) + b.astype(F32)).astype(BF)


def project_body(x_ref, w_ref, b_ref, tq_ref, tkv_ref):
    y = (nn(x_ref[...], w_ref[...]) + b_ref[...]).astype(BF)
    for t in range(2):
        for lo in range(4):
            tq_ref[t, :, lo * DH : (lo + 1) * DH] = y[
                lo * 128 : (lo + 1) * 128, t * DH : (t + 1) * DH
            ]
        for lo in range(2):
            tkv_ref[t, :, lo * 128 : (lo + 1) * 128] = y[
                lo * 256 : (lo + 1) * 256, (t + 1) * 128 : (t + 2) * 128
            ]


def project(x_all, w_sel, b_sel):
    blocks = x_all.shape[0] // 512
    width = x_all.shape[1]
    return pl.pallas_call(
        project_body,
        grid=(blocks,),
        in_specs=[
            pl.BlockSpec((512, width), lambda j: (j, 0)),
            pl.BlockSpec((width, 384), lambda j: (0, 0)),
            pl.BlockSpec((1, 384), lambda j: (0, 0)),
        ],
        out_specs=[
            pl.BlockSpec((2, 128, 256), lambda j: (0, j, 0)),
            pl.BlockSpec((2, 256, 256), lambda j: (0, j, 0)),
        ],
        out_shape=[
            jax.ShapeDtypeStruct((2, 1024, 256), BF),
            jax.ShapeDtypeStruct((2, 2048, 256), BF),
        ],
        compiler_params=pltpu.CompilerParams(vmem_limit_bytes=VMEM),
        name="project",
        cost_estimate=cost(1),
    )(x_all, w_sel, b_sel)


def hot_rows(col, count):
    lane = lax.broadcasted_iota(jnp.int32, (1, count), 1).astype(jnp.int16)
    shape = (col.shape[0], count)
    same = jnp.broadcast_to(lane, shape) == jnp.broadcast_to(col.astype(jnp.int16), shape)
    return jnp.where(same, jnp.ones((), BF), jnp.zeros((), BF))


def hot_cols(row, count):
    place = lax.broadcasted_iota(jnp.int32, (count, 1), 0).astype(jnp.int16)
    shape = (count, row.shape[1])
    same = jnp.broadcast_to(place, shape) == jnp.broadcast_to(row.astype(jnp.int16), shape)
    return jnp.where(same, jnp.ones((), BF), jnp.zeros((), BF))


def take_quarter(table, place):
    wide = nn(hot_rows(place & 1023, 1024), table)
    lane = lax.broadcasted_iota(jnp.int32, wide.shape, 1)
    wide = jnp.where((lane >> 6) == (place >> 10), wide, 0.0)
    half = wide[:, :128] + wide[:, 128:]
    return half + pltpu.roll(half, 64, 1)


def take_half(table, place):
    wide = nn(hot_rows(place & 2047, 2048), table)
    return jnp.where((place >> 11) == 1, wide[:, 128:], wide[:, :128])


def spread_quarter(twice, place):
    wide = jnp.concatenate([twice, twice], 1)
    lane = lax.broadcasted_iota(jnp.int32, wide.shape, 1)
    return jnp.where((lane >> 6) == (place >> 10), wide, 0.0).astype(BF)


def spread_half(rows, place):
    upper = (place >> 11) == 1
    return jnp.concatenate(
        [jnp.where(upper, 0.0, rows), jnp.where(upper, rows, 0.0)], 1
    ).astype(BF)


def low_lanes(shape):
    return lax.broadcasted_iota(jnp.int32, shape, 1) < DH


def attend_body(
    pq_ref, pk_ref, pqr_ref, tq_ref, tkv_ref, q_ref, kv_ref, lt_ref, ent_ref, out_ref, acc_ref, got_ref
):
    step = pl.program_id(0)
    place_q = pq_ref[0]
    twice = take_quarter(tq_ref[0], place_q)
    q_all = jnp.where(low_lanes(twice.shape), twice, 0.0).astype(BF)
    kv_all = take_half(tkv_ref[0], pk_ref[0]).astype(BF)
    q_ref[0] = q_all
    kv_ref[0] = kv_all

    def cluster(c, rows):
        kv = kv_ref[0, rows, :]
        scores = nt(q_ref[0, rows, :], kv) * (DH**-0.5)
        top = jnp.max(scores, 1, keepdims=True)
        total = jnp.sum(jnp.exp(scores - top), 1, keepdims=True)
        log_total = top + jnp.log(total)
        soft = jnp.exp(scores - log_total)
        inner = jnp.sum(soft * scores, 1, keepdims=True)
        ent_ref[0, pl.ds(c, 1), :] = jnp.broadcast_to(
            jnp.sum(log_total - inner, 0, keepdims=True) / CLUSTER, (1, 128)
        )
        lt_ref[0, rows, :] = log_total
        got = nn(soft.astype(BF), kv)
        got_ref[rows, :] = jnp.where(low_lanes(got.shape), pltpu.roll(got, 64, 1), got)

    clusters(cluster)
    spread = spread_quarter(got_ref[...], place_q)

    @pl.when((step == 0) | (step == FULL_STEPS))
    def _():
        acc_ref[...] = jnp.zeros(acc_ref.shape, F32)

    acc_ref[...] += nn(hot_cols(pqr_ref[0] & 1023, 1024), spread)

    @pl.when((step == FULL_STEPS - 1) | (step == STEPS - 1))
    def _():
        rows = pl.ds(pl.multiple_of(128 * table_of(step), 128), 128)
        for j in range(out_ref.shape[0]):
            out_ref[j, rows, :] = acc_ref[j * 128 : (j + 1) * 128, :].astype(BF)


def table_of(g):
    return g // FULL_STEPS


def once(*shape):
    return pl.BlockSpec(shape, lambda g: (0,) * len(shape))


def attend(places, tq, tkv):
    pq_col, pk_col, pq_row, _ = places
    chunk = lambda width: pl.BlockSpec((1, CHUNK, width), lambda g: (g, 0, 0))
    table = lambda rows: pl.BlockSpec((1, rows, 256), lambda g: (table_of(g), 0, 0))
    return pl.pallas_call(
        attend_body,
        grid=(STEPS,),
        in_specs=[
            chunk(1),
            chunk(1),
            pl.BlockSpec((1, 1, CHUNK), lambda g: (g, 0, 0)),
            table(1024),
            table(2048),
        ],
        out_specs=[
            chunk(128),
            chunk(128),
            chunk(1),
            pl.BlockSpec((1, 8, 128), lambda g: (g, 0, 0)),
            once(8, 256, 256),
        ],
        out_shape=[
            jax.ShapeDtypeStruct((STEPS, CHUNK, 128), BF),
            jax.ShapeDtypeStruct((STEPS, CHUNK, 128), BF),
            jax.ShapeDtypeStruct((STEPS, CHUNK, 1), F32),
            jax.ShapeDtypeStruct((STEPS, 8, 128), F32),
            jax.ShapeDtypeStruct((8, 256, 256), BF),
        ],
        scratch_shapes=[pltpu.VMEM((1024, 256), F32), pltpu.VMEM((CHUNK, 128), F32)],
        compiler_params=pltpu.CompilerParams(vmem_limit_bytes=VMEM),
        name="attend",
        cost_estimate=cost(1),
    )(pq_col, pk_col, pq_row, tq, tkv)


def attend_back_body(
    pq_ref, pk_ref, pqr_ref, pkr_ref, td_ref, q_ref, kv_ref, lt_ref, out_ref, accq, acckv, d_ref, gq_ref, gkv_ref
):
    step = pl.program_id(0)
    place_q = pq_ref[0]
    twice = take_quarter(td_ref[...], place_q)
    d_ref[...] = jnp.where(low_lanes(twice.shape), 0.0, twice).astype(BF)

    def cluster(c, rows):
        q = q_ref[0, rows, :]
        kv = kv_ref[0, rows, :]
        d = d_ref[rows, :]
        scores = nt(q, kv) * (DH**-0.5)
        soft = jnp.exp(scores - lt_ref[0, rows, :])
        d_soft = nt(d, kv)
        d_scores = soft * (d_soft - jnp.sum(soft * d_soft, 1, keepdims=True))
        d_raw = (d_scores * (DH**-0.5)).astype(BF)
        got = nn(d_raw, kv)
        gq_ref[rows, :] = jnp.where(low_lanes(got.shape), got, pltpu.roll(got, 64, 1))
        gkv_ref[rows, :] = tn(d_raw, q) + tn(soft.astype(BF), d)

    clusters(cluster)

    @pl.when(step == 0)
    def _():
        accq[...] = jnp.zeros(accq.shape, F32)
        acckv[...] = jnp.zeros(acckv.shape, F32)

    accq[...] += nn(hot_cols(pqr_ref[0] & 1023, 1024), spread_quarter(gq_ref[...], place_q))
    acckv[...] += nn(hot_cols(pkr_ref[0] & 2047, 2048), spread_half(gkv_ref[...], pk_ref[0]))

    @pl.when(step == pl.num_programs(0) - 1)
    def _():
        for j in range(out_ref.shape[0]):
            out_ref[j, :128, :] = accq[j * 128 : (j + 1) * 128, :].astype(BF)
            out_ref[j, 128:, :] = acckv[j * 256 : (j + 1) * 256, :].astype(BF)


def attend_back(places, start, steps, td, q_all, kv_all, log_total):
    pq_col, pk_col, pq_row, pk_row = places
    chunk = lambda width: pl.BlockSpec((1, CHUNK, width), lambda g: (g + start, 0, 0))
    col = chunk(1)
    line = pl.BlockSpec((1, 1, CHUNK), lambda g: (g + start, 0, 0))
    return pl.pallas_call(
        attend_back_body,
        grid=(steps,),
        in_specs=[
            col,
            col,
            line,
            line,
            once(1024, 256),
            chunk(128),
            chunk(128),
            chunk(1),
        ],
        out_specs=once(8, 384, 256),
        out_shape=jax.ShapeDtypeStruct((8, 384, 256), BF),
        scratch_shapes=[
            pltpu.VMEM((1024, 256), F32),
            pltpu.VMEM((2048, 256), F32),
            pltpu.VMEM((CHUNK, 128), BF),
            pltpu.VMEM((CHUNK, 128), F32),
            pltpu.VMEM((CHUNK, 128), F32),
        ],
        compiler_params=pltpu.CompilerParams(vmem_limit_bytes=VMEM),
        name="attend_back",
        cost_estimate=cost(1),
    )(pq_col, pk_col, pq_row, pk_row, td, q_all, kv_all, log_total)


def project_grad_body(x_ref, full_ref, half_ref, grad_ref, sum_ref, acc_ref):
    j = pl.program_id(0)
    quarters = []
    for lo in range(4):
        cols = slice(lo * DH, (lo + 1) * DH)
        quarters.append(jnp.concatenate([full_ref[0, :128, cols], half_ref[0, :128, cols]], 1))
    parts = [jnp.concatenate(quarters, 0)]
    for ref in (full_ref, half_ref):
        parts.append(jnp.concatenate([ref[0, 128:, :128], ref[0, 128:, 128:]], 0))
    rows = jnp.concatenate(parts, 1)
    part = tn(x_ref[...], rows)
    sums = jnp.sum(rows.astype(F32), 0, keepdims=True)

    @pl.when(j == 0)
    def _():
        acc_ref[...] = part
        sum_ref[...] = sums

    @pl.when(j > 0)
    def _():
        acc_ref[...] += part
        sum_ref[...] += sums

    @pl.when(j == pl.num_programs(0) - 1)
    def _():
        grad_ref[...] = acc_ref[...].astype(BF)


def project_grad(x_all, full, half):
    tokens, width = x_all.shape
    rows = pl.BlockSpec((1, 384, 256), lambda j: (j, 0, 0))
    return pl.pallas_call(
        project_grad_body,
        grid=(tokens // 512,),
        in_specs=[pl.BlockSpec((512, width), lambda j: (j, 0)), rows, rows],
        out_specs=[once(width, 384), once(1, 384)],
        out_shape=[
            jax.ShapeDtypeStruct((width, 384), BF),
            jax.ShapeDtypeStruct((1, 384), F32),
        ],
        scratch_shapes=[pltpu.VMEM((width, 384), F32)],
        compiler_params=pltpu.CompilerParams(vmem_limit_bytes=VMEM),
        name="project_grad",
        cost_estimate=cost(1),
    )(x_all, full, half)


def project_back_body(heads, full_ref, half_ref, w_ref, dfi_ref, dx_ref, q_ref, kv_ref, wq_ref, wkv_ref):
    for hd in range(heads):
        wq_ref[hd * 3 * DH : (hd + 1) * 3 * DH, :] = w_ref[hd, : 3 * DH, :]
        wkv_ref[hd * 6 * DH : (hd + 1) * 6 * DH, :] = w_ref[hd, 3 * DH :, :]
        for h in range(3):
            if h == 1:
                piece = (half_ref[hd].astype(F32) + half_ref[heads + hd].astype(F32)).astype(BF)
            else:
                piece = full_ref[(h // 2) * heads + hd]
            n = hd * 3 + h
            for lo in range(4):
                q_ref[lo * 128 : (lo + 1) * 128, n * DH : (n + 1) * DH] = piece[
                    :128, lo * DH : (lo + 1) * DH
                ]
            for lo in range(2):
                kv_ref[lo * 256 : (lo + 1) * 256, n * 128 : (n + 1) * 128] = piece[
                    128:, lo * 128 : (lo + 1) * 128
                ]

    def back(cols):
        dx = dfi_ref[:, cols] + nn(q_ref[...], wq_ref[:, cols]) + nn(kv_ref[...], wkv_ref[:, cols])
        dx_ref[:, cols] = dx.astype(BF)

    columns(dx_ref.shape[1], back)


def project_back(full, half, w_all, d_first_in):
    tokens, width = d_first_in.shape
    heads = w_all.shape[0]
    return pl.pallas_call(
        functools.partial(project_back_body, heads),
        out_shape=jax.ShapeDtypeStruct((tokens, width), BF),
        scratch_shapes=[
            pltpu.VMEM((tokens, width), BF),
            pltpu.VMEM((tokens, 2 * width), BF),
            pltpu.VMEM((width, width), BF),
            pltpu.VMEM((2 * width, width), BF),
        ],
        compiler_params=pltpu.CompilerParams(vmem_limit_bytes=VMEM),
        name="project_back",
        cost_estimate=cost(1),
    )(full, half, w_all, d_first_in)


def erf_parts(u):
    mag = jnp.abs(u) * (0.5**0.5)
    bell = jnp.exp(-(mag * mag))
    t = 1.0 / (1.0 + 0.3275911 * mag)
    poly = t * (
        0.254829592
        + t * (-0.284496736 + t * (1.421413741 + t * (-1.453152027 + t * 1.061405429)))
    )
    tail = 0.5 * poly * bell
    return jnp.where(u < 0, tail, 1.0 - tail), bell * ((2 * jnp.pi) ** -0.5)


def row_mean(x):
    return jnp.mean(x, 1, keepdims=True)


def column_sum(x):
    return jnp.sum(x, 0, keepdims=True)


def middle_body(
    heads,
    hc_ref,
    got_ref,
    x_ref,
    dout_ref,
    mask_ref,
    wo_ref,
    up_ref,
    down_ref,
    bias_ref,
    gain_ref,
    shift_ref,
    res_ref,
    send_full_ref,
    send_half_ref,
    dfi_ref,
    down_sent_ref,
    down_kept_ref,
    up_sent_ref,
    up_kept_ref,
    sums_ref,
    gbup_ref,
    rows_ref,
    n1_ref,
    inv1_ref,
    low_ref,
    low_t_ref,
    acc_ref,
    hid_ref,
    slope_ref,
    dlow_ref,
    dlow_t_ref,
    dup_ref,
    rows_back_ref,
):
    step = pl.program_id(0)
    tokens, width = x_ref.shape
    hid = up_ref.shape[2]
    size = 64

    def tiles(body, carry):
        def at(i, carry):
            return body(pl.ds(pl.multiple_of(i * size, size), size), carry)

        return lax.fori_loop(0, tokens // size, at, carry)

    @pl.when(step == 0)
    def _():
        for hd in range(heads):
            rows_ref[:, hd * 256 + 3 * DH : (hd + 1) * 256] = jnp.zeros((tokens, DH), BF)
            for h in range(3):
                if h == 1:
                    piece = plus(got_ref[hd, 128:, :], got_ref[heads + hd, 128:, :])
                else:
                    piece = got_ref[hd + (h // 2) * heads, :128, :]
                col = hd * 256 + h * DH
                for lo in range(4):
                    rows_ref[lo * 128 : (lo + 1) * 128, col : col + DH] = piece[
                        :, lo * DH : (lo + 1) * DH
                    ]

        def project(cols):
            acc_ref[:, cols] = nn(rows_ref[...], wo_ref[:, cols])

        columns(width, project)

        def norm(r, carry):
            v = x_ref[r, :].astype(F32) + acc_ref[r, :] + bias_ref[0:1, :]
            centred = v - row_mean(v)
            inv = lax.rsqrt(row_mean(centred * centred) + EPS)
            normed = centred * inv
            first = normed * gain_ref[0:1, :] + shift_ref[0:1, :]
            n1_ref[r, :] = normed
            inv1_ref[r, :] = inv
            low_ref[r, :] = first.astype(BF)
            acc_ref[r, :] = first + bias_ref[1:2, :]
            return carry

        tiles(norm, 0)
        low_t_ref[...] = low_ref[...].T

    @pl.when(step < heads)
    def _():
        at_bias = pl.multiple_of(chunk_at(step, heads, hc_ref[0]) * 256 + 3 * DH, DH)

        def upper(cols):
            bup = wo_ref[pl.ds(at_bias, 16), cols][:1].astype(F32)
            u = nn(low_ref[...], up_ref[0, :, cols]) + bup
            phi, bell = erf_parts(u)
            hid_ref[step, :, cols] = (u * phi).astype(BF)
            slope_ref[step, :, cols] = phi + u * bell

        columns(hid, upper)
        acc_ref[...] += nn(hid_ref[step], down_ref[0])

    @pl.when(step == heads)
    def _():
        zero = jnp.zeros((1, width), F32)

        def norm(r, carry):
            g_sum, s_sum, b_sum = carry
            v = acc_ref[r, :]
            centred = v - row_mean(v)
            inv = lax.rsqrt(row_mean(centred * centred) + EPS)
            normed = centred * inv
            res_ref[r, :] = (normed * gain_ref[1:2, :] + shift_ref[1:2, :]).astype(BF)
            seed = dout_ref[r, :].astype(F32) * mask_ref[r, :]
            e = seed * gain_ref[1:2, :]
            d = inv * (e - row_mean(e) - normed * row_mean(e * normed))
            acc_ref[r, :] = d
            dlow_ref[r, :] = d.astype(BF)
            return g_sum + column_sum(seed * normed), s_sum + column_sum(seed), b_sum + column_sum(d)

        g_sum, s_sum, b_sum = tiles(norm, (zero, zero, zero))
        sums_ref[1:2, :] = b_sum
        sums_ref[3:4, :] = g_sum
        sums_ref[5:6, :] = s_sum
        dlow_t_ref[...] = dlow_ref[...].T

    @pl.when(step >= heads)
    def _():
        c = step - heads
        for n in range(0, hid, 256):
            cols = slice(n, n + 256)
            d_up = nt(dlow_ref[...], down_ref[0, cols, :]) * slope_ref[c, :, cols]
            gbup_ref[0, :, cols] = column_sum(d_up)
            dup_ref[:, cols] = d_up.astype(BF)

        acc_ref[...] += nt(dup_ref[...], up_ref[0])

        for there, k, down_to, up_to in (
            (c < heads // 2, c, down_sent_ref, up_sent_ref),
            (c >= heads // 2, c - heads // 2, down_kept_ref, up_kept_ref),
        ):

            @pl.when(there)
            def _():
                def products(cols):
                    down_to[k, :, cols] = nn(dlow_t_ref[...], hid_ref[c, :, cols]).astype(BF)
                    up_to[k, :, cols] = nn(low_t_ref[...], dup_ref[:, cols]).astype(BF)

                columns(hid, products)

    @pl.when(step == 2 * heads - 1)
    def _():
        zero = jnp.zeros((1, width), F32)

        def norm(r, carry):
            g_sum, s_sum, b_sum = carry
            d_first = acc_ref[r, :]
            normed = n1_ref[r, :]
            e = d_first * gain_ref[0:1, :]
            d = inv1_ref[r, :] * (e - row_mean(e) - normed * row_mean(e * normed))
            dfi_ref[r, :] = d
            dlow_ref[r, :] = d.astype(BF)
            return (
                g_sum + column_sum(d_first * normed),
                s_sum + column_sum(d_first),
                b_sum + column_sum(d),
            )

        g_sum, s_sum, b_sum = tiles(norm, (zero, zero, zero))
        sums_ref[0:1, :] = b_sum
        sums_ref[2:3, :] = g_sum
        sums_ref[4:5, :] = s_sum
        dlow_t_ref[...] = dlow_ref[...].T

        def back(cols):
            rows_back_ref[:, cols] = nt(dlow_ref[...], wo_ref[cols, :]).astype(BF)

        columns(heads * 256, back)
        for lo in range(4):
            for hd in range(heads):
                for h in range(3):
                    col = hd * 256 + h * DH
                    piece = rows_back_ref[lo * 128 : (lo + 1) * 128, col : col + DH]
                    lanes = slice(lo * DH, (lo + 1) * DH)
                    if h == 1:
                        send_half_ref[hd, :, lanes] = piece
                        send_half_ref[heads + hd, :, lanes] = piece
                    else:
                        send_full_ref[hd + (h // 2) * heads, :, lanes] = piece

        def grad(k, carry):
            at = pl.multiple_of(chunk_at(k, heads, hc_ref[0]) * 256, 256)
            whole = nn(dlow_t_ref[...], rows_ref[:, pl.ds(at, 256)]).astype(BF)

            @pl.when(k < heads // 2)
            def _():
                down_sent_ref[k, :, hid:] = whole[:, :SIDE]
                up_sent_ref[k, :, hid:] = whole[:, SIDE:]

            @pl.when(k >= heads // 2)
            def _():
                down_kept_ref[k - heads // 2, :, hid:] = whole[:, :SIDE]
                up_kept_ref[k - heads // 2, :, hid:] = whole[:, SIDE:]

            return carry

        lax.fori_loop(0, heads, grad, 0)


def chunk_at(k, heads, hc):
    pairs = heads // 2
    return jnp.where(k < pairs, 2 * k + 1 - hc, 2 * (k - pairs) + hc)


def middle(hc, got, x_own, d_own, mask_col, wo, ff_all, bias, gain, shift):
    heads, width, hid = ff_all.shape[0], ff_all.shape[2], ff_all.shape[1] - ff_all.shape[2]
    pairs = heads // 2
    tokens = x_own.shape[0]

    def at(k, hc_ref):
        return chunk_at(k, heads, hc_ref[0])

    once = lambda *shape: pl.BlockSpec(shape, lambda g, c: (0,) * len(shape))
    by_chunk = lambda part, *shape: pl.BlockSpec(shape, lambda g, c: (at(g % heads, c), part, 0))
    late = lambda *shape: pl.BlockSpec(shape, lambda g, c: (at(jnp.maximum(g - heads, 0), c), 0, 0))
    grads = pl.BlockSpec(
        (pairs, width, hid + SIDE), lambda g, c: (0, 0, 0), pipeline_mode=pl.Buffered(1)
    )
    big = jax.ShapeDtypeStruct((pairs, width, hid + SIDE), BF)
    table = jax.ShapeDtypeStruct((OWN * heads, 128, 256), BF)
    return pl.pallas_call(
        functools.partial(middle_body, heads),
        grid_spec=pltpu.PrefetchScalarGridSpec(
            num_scalar_prefetch=1,
            grid=(2 * heads,),
            in_specs=[
                once(OWN * heads, 256, 256),
                once(tokens, width),
                once(tokens, width),
                once(tokens, 1),
                once(heads * 256, width),
                by_chunk(0, 1, width, hid),
                by_chunk(1, 1, hid, width),
                once(2, width),
                once(2, width),
                once(2, width),
            ],
            out_specs=[
                once(tokens, width),
                once(OWN * heads, 128, 256),
                once(OWN * heads, 128, 256),
                once(tokens, width),
                grads,
                grads,
                grads,
                grads,
                once(8, width),
                late(1, 1, hid),
            ],
            scratch_shapes=[
                pltpu.VMEM((tokens, heads * 256), BF),
                pltpu.VMEM((tokens, width), F32),
                pltpu.VMEM((tokens, 1), F32),
                pltpu.VMEM((tokens, width), BF),
                pltpu.VMEM((width, tokens), BF),
                pltpu.VMEM((tokens, width), F32),
                pltpu.VMEM((heads, tokens, hid), BF),
                pltpu.VMEM((heads, tokens, hid), F32),
                pltpu.VMEM((tokens, width), BF),
                pltpu.VMEM((width, tokens), BF),
                pltpu.VMEM((tokens, hid), BF),
                pltpu.VMEM((tokens, heads * 256), BF),
            ],
        ),
        out_shape=[
            jax.ShapeDtypeStruct((tokens, width), BF),
            table,
            table,
            jax.ShapeDtypeStruct((tokens, width), F32),
            big,
            big,
            big,
            big,
            jax.ShapeDtypeStruct((8, width), F32),
            jax.ShapeDtypeStruct((heads, 1, hid), F32),
        ],
        compiler_params=pltpu.CompilerParams(vmem_limit_bytes=VMEM),
        name="middle",
        cost_estimate=cost(1),
    )(hc, got, x_own, d_own, mask_col, wo, ff_all, ff_all, bias, gain, shift)


def swap(x, axis, bit=1):
    size = lax.axis_size(axis)
    return lax.ppermute(x, axis, [(i, i ^ bit) for i in range(size)])


def pick(x, index, axis=0):
    return lax.dynamic_index_in_dim(x, index, axis, keepdims=False)


def fold(kept, came, index, axis):
    return tuple(plus(pick(kept, i, axis), pick(came, i, axis)) for i in (1 - index, index))


def total(pieces):
    return sum(p.astype(F32) for p in pieces)


barrier = lax.optimization_barrier


def per_device(
    inputs,
    w_qkv,
    b_qv,
    w_out,
    out_bias,
    w_up,
    b_up,
    w_down,
    norm_gain,
    norm_shift,
    d_out,
    q_perm,
    k_perm,
    masked,
):
    seqs, block_len, width = inputs.shape
    heads = lax.axis_size("hx") * lax.axis_size("hc")
    plane = OWN * heads
    share = block_len // heads
    tokens = seqs * share
    length = lax.axis_size("sq") * OWN
    sq = lax.axis_index("sq")
    own = lax.axis_index("own")
    hx = lax.axis_index("hx")
    hc = lax.axis_index("hc")
    head = hx * lax.axis_size("hc") + hc
    head_cols = q_perm.shape[1] * DH

    pad = jnp.zeros((256 - head_cols - 1, width), BF)
    with_bias = jnp.concatenate([w_out, b_up[None], pad], 0)
    mine = lax.dynamic_slice_in_dim(inputs, head * share, share, 1)
    x_own = lax.all_to_all(mine, "sq", 0, 0, tiled=True).reshape(tokens, width)
    out_bias_all = lax.all_gather(with_bias, HEAD, axis=0, tiled=False)
    x_own, out_bias_all, d_out, q_perm, k_perm, w_qkv = barrier(
        (x_own, out_bias_all, d_out, q_perm, k_perm, w_qkv)
    )
    x_all = lax.all_gather(x_own, PLANE, axis=0, tiled=True)
    d_own = lax.all_to_all(d_out, "sq", 0, 0, tiled=True).reshape(tokens, width)

    def positions(perm):
        mine = pick(perm, sq)
        full = pick(mine, 2 * own).reshape(2, TOK_DEV)
        half = lax.dynamic_slice_in_dim(mine[1], own * TOK_DEV, TOK_DEV, 0)
        return jnp.concatenate([full, half[None]], 0).reshape(-1, 1, CHUNK)

    masked_row = pick(masked, sq)
    *places, mask_col, listed = prepare(
        block_len,
        heads,
        jnp.stack([own, head]).astype(jnp.int32),
        positions(q_perm),
        positions(k_perm),
        lax.dynamic_slice_in_dim(pick(q_perm, sq), own * TOK_DEV, TOK_DEV, 1).reshape(-1, 1, CHUNK),
        masked_row[None],
        tokens,
    )

    def two_heads(x):
        full = lax.dynamic_slice_in_dim(x, own * 2 * DH, DH, x.ndim - 1)
        return full, x[..., DH : 2 * DH]

    w_full, w_half = two_heads(w_qkv)
    w_sel = jnp.concatenate(
        [w_full[0], w_half[0], w_full[1], w_full[2], w_half[1], w_half[2]], 1
    )
    b_full, b_half = two_heads(b_qv.astype(F32))
    none = jnp.zeros((DH,), F32)
    b_sel = jnp.concatenate([b_full[0], b_half[0], none, b_full[1], none, b_half[1]])[None]
    w_rows = jnp.concatenate(
        [w_qkv[0]]
        + [w_qkv[i, :, h * DH : (h + 1) * DH] for h in range(3) for i in (1, 2)],
        1,
    ).T
    ff = jnp.concatenate([w_up, w_down], 0)

    occupancy = jnp.sum(listed.reshape(q_perm.shape[1], TOK_DEV // CLUSTER, CLUSTER), -1)
    bias = out_bias.astype(F32)
    out_all = out_bias_all.reshape(heads * 256, width)

    (
        x_all,
        d_own,
        places,
        w_sel,
        b_sel,
        w_rows,
        mask_col,
        occupancy,
        bias,
        out_all,
        ff,
    ) = barrier(
        (
            x_all,
            d_own,
            places,
            w_sel,
            b_sel,
            w_rows,
            mask_col,
            occupancy,
            bias,
            out_all,
            ff,
        )
    )
    ff_all = lax.all_gather(ff, HEAD, axis=0, tiled=False)

    tq, tkv = project(x_all, w_sel, b_sel)
    *kept, ent, done = attend(places, tq, tkv)
    got = lax.all_to_all(done, PLANE, 0, 0, tiled=True)
    ent_seg = ent[:, :GROUPS, 0].reshape(3, TOK_DEV // CLUSTER)
    ent_got = swap(jnp.where(own == 0, ent_seg[1], ent_seg[0]), "own")
    ff_all, w_rows, got = barrier((ff_all, w_rows, got))
    w_all = lax.all_gather(w_rows, HEAD, axis=0, tiled=False)
    (
        result_own,
        send_full,
        send_half,
        d_first_in,
        down_sent,
        down_kept,
        up_sent,
        up_kept,
        sums_own,
        grad_bup,
    ) = middle(
        hc[None],
        got,
        x_own,
        d_own,
        mask_col,
        out_all,
        ff_all,
        bias,
        norm_gain,
        norm_shift,
    )
    rows = width // length
    near = seqs <= 4

    def shifted(pieces):
        return [pieces[0]] + [
            lax.ppermute(p, "sq", [(i, (i + s) % seqs) for i in range(seqs)])
            for s, p in enumerate(pieces)
            if s > 0
        ]

    def cut_z(x):
        return [pick(x, (sq + s) % seqs) for s in range(seqs)] if near else [x]

    def over_z(pieces):
        if near:
            return shifted(pieces)
        return list(lax.all_to_all(pieces[0], "sq", 0, 0, tiled=True))

    td_full = lax.all_to_all(send_full, PLANE, 0, 0, tiled=True)
    down_came, up_came = swap(down_sent, "hc"), swap(up_sent, "hc")
    result_own = cut_z(result_own.reshape(seqs, share, width))
    cut = lambda x: x.reshape(x.shape[0], length // OWN, OWN, rows, x.shape[-1])
    down_sent, down_kept = fold(cut(down_kept), cut(down_came), hx, 0)
    up_sent, up_kept = fold(cut(up_kept), cut(up_came), own, 2)
    (
        td_full,
        send_half,
        ent_got,
        w_all,
        down_sent,
        down_kept,
        up_sent,
        up_kept,
        result_own,
    ) = barrier(
        (
            td_full,
            send_half,
            ent_got,
            w_all,
            down_sent,
            down_kept,
            up_sent,
            up_kept,
            result_own,
        )
    )
    td_half = lax.all_to_all(send_half, PLANE, 0, 0, tiled=True)
    down_came, up_came = swap(down_sent, "hx"), swap(up_sent, "own")
    result_got = over_z(result_own)
    rows_full = attend_back(places, 0, FULL_STEPS, td_full.reshape(plane * 128, 256), *kept)
    rows_full, td_half, down_came, up_came, result_got = barrier(
        (rows_full, td_half, down_came, up_came, result_got)
    )
    back_full = lax.all_to_all(rows_full, PLANE, 0, 0, tiled=True)
    down_sent, down_kept = fold(down_kept, down_came, own, 1)
    up_sent, up_kept = fold(up_kept, up_came, hx, 0)
    td_half, down_sent, down_kept, up_sent, up_kept = barrier(
        (td_half, down_sent, down_kept, up_sent, up_kept)
    )
    down_came, up_came = swap(down_sent, "own"), swap(up_sent, "hx")
    rows_half = attend_back(
        places, FULL_STEPS, STEPS - FULL_STEPS, td_half.reshape(plane * 128, 256), *kept
    )
    rows_half, back_full = barrier((rows_half, back_full))
    back_half = lax.all_to_all(rows_half, PLANE, 0, 0, tiled=True)
    rows_half, down_came, up_came = barrier((rows_half, down_came, up_came))
    both = cut_z(jnp.concatenate([plus(down_kept, down_came), plus(up_kept, up_came)], 2))
    rows_full, rows_half, both = barrier((rows_full, rows_half, both))
    both_got = over_z(both)
    grad_sel, sum_sel = project_grad(x_all, rows_full, rows_half)

    sums = sum_sel.reshape(6, DH)
    at_full = (jnp.arange(3) == 2 * own)[:, None]
    at_half = (jnp.arange(3) == 1)[:, None]
    at_head = (jnp.arange(heads) == head)[None, :, None, None]
    pair = jnp.stack(
        [jnp.where(at_full, sums[a], 0.0) + jnp.where(at_half, sums[b], 0.0) for a, b in ((0, 1), (3, 5))]
    )
    bqv = jnp.where(at_head, pair[:, None], 0.0)
    small = jnp.concatenate([sums_own[:6].reshape(-1), grad_bup.reshape(-1), bqv.reshape(-1)])
    grad_sel = grad_sel.reshape(length // OWN, OWN, rows, 384)
    grad_sent, grad_kept = pick(grad_sel, 1 - own, 1), pick(grad_sel, own, 1)
    grad_came = swap(grad_sent, "own")
    back_half, grad_came = barrier((back_half, grad_came))
    low = jnp.where(own == 0, grad_kept, grad_came)
    high = jnp.where(own == 0, grad_came, grad_kept)
    shared = plus(grad_kept, grad_came)
    order = [(low, 0), (shared, 1), (high, 0), (low, 2), (shared, 4), (high, 2), (low, 3), (shared, 5), (high, 3)]
    grad_all = cut_z(jnp.concatenate([a[..., c * DH : (c + 1) * DH] for a, c in order], -1))
    back_full, grad_all = barrier((back_full, grad_all))
    grad_got = over_z(grad_all)
    d_in_own = project_back(back_full, back_half, w_all, d_first_in)
    d_in_own, small = barrier((d_in_own, small))
    for axis in ("hc", "hx", "own"):
        small = small + swap(small, axis)
    bit = 1
    while bit < seqs:
        small = small + swap(small, "sq", bit)
        bit *= 2
    d_inputs = lax.all_to_all(
        d_in_own.reshape(seqs, share, width), "sq", 0, 0, tiled=True
    ).astype(F32)
    both = total(both_got)
    wide = both.shape[1] // 2
    down_sum = both[:, : wide - SIDE]
    up_sum = both[:, wide : 2 * wide - SIDE]
    out_sum = jnp.concatenate([both[:, wide - SIDE : wide], both[:, 2 * wide - SIDE :]], 1)[:, :head_cols]
    qkv_sum = total(grad_got).reshape(rows, 3, head_cols).transpose(1, 0, 2)
    if near:
        parts = []
        for i in range(seqs):
            part = result_got[0]
            for s in range(1, seqs):
                part = jnp.where((i + s) % seqs == sq, result_got[s], part)
            parts.append(part)
        result = jnp.stack(parts)
    else:
        result = jnp.stack(result_got)

    obias_sum = small[: 2 * width].reshape(2, width)
    gain_sum = small[2 * width : 4 * width].reshape(2, width)
    shift_sum = small[4 * width : 6 * width].reshape(2, width)
    bup_sum = small[6 * width : -2 * width]
    bqv_sum = small[-2 * width :].reshape(2, width)

    entropy = jnp.stack(
        [
            jnp.where(own == 0, ent_seg[0], ent_got),
            ent_seg[2],
            jnp.where(own == 0, ent_got, ent_seg[1]),
        ]
    )
    return (
        result.astype(F32),
        d_inputs,
        qkv_sum,
        bqv_sum,
        out_sum.T,
        obias_sum,
        up_sum,
        bup_sum,
        down_sum.T,
        gain_sum,
        shift_sum,
        entropy,
        occupancy,
    )


def solution(mesh):
    seq, head = (mesh.shape["seq"], mesh.shape["head"])
    fine = Mesh(
        mesh.devices.reshape(seq // OWN, OWN, 2, head // 2), ("sq", "own", "hx", "hc")
    )
    both = SEQ + HEAD
    placed = (
        P(None, SEQ, None),
        P(None, None, HEAD),
        P(None, HEAD),
        P(HEAD, None),
        P(),
        P(None, HEAD),
        P(HEAD),
        P(HEAD, None),
        P(),
        P(),
        P(None, both, None),
        P(None, HEAD, None),
        P(None, HEAD, None),
        P(),
    )
    return jax.shard_map(
        per_device,
        mesh=fine,
        in_specs=placed,
        out_specs=(
            P(None, both, None),
            P(None, both, None),
            P(None, SEQ, HEAD),
            P(),
            P(HEAD, SEQ),
            P(),
            P(SEQ, HEAD),
            P(),
            P(HEAD, SEQ),
            P(),
            P(),
            P(HEAD, SEQ),
            P(HEAD, SEQ),
        ),
        check_vma=False,
    )
```

profile of v0, /device:TPU:0, one launch (start us, length us, event | category | flops | bytes accessed | tf_op | source)
XLA Modules:
  0.0 389.0 jit_solution(2337423483414312459)
XLA Ops:
  10.2 26.5 %all_to_all.40 = bf16[4,128,768]{2,1,0:T(8,128)(2,1)} all-to-all(bf16[4,128,768]{2,1,0:T(8,128)(2,1)S(1)} %constant_dynamic-slice_fusion.7), channel_id=1, replica_groups=mesh['sq'=4,'own'=2,'hx'=2,'hc'=2] {'sq'}, dimensions={0} | all-to-all | bytes 1572864 | tf_op jit(solution)/shard_map/all_to_all | solution.py:835
  40.1 2.9 pad_maximum_fusion
  46.9 3.5 all-to-all-start.1
  54.0 10.7 %prepare.1 = (s32[12,512,1]{2,1,0:T(8,128)}, s32[12,512,1]{2,1,0:T(8,128)}, s32[12,1,512]{2,1,0:T(1,128)}, s32[12,1,512]{2,1,0:T(1,128)}, f32[512,1]{1,0:T(8,128)}, /*index=5*/s32[12,1,512]{2,1,0:T(1,128)}) custom-call(s32[2]{0:T(128)} %pad_add_fusion.2.here_ref, s32[12,1,512]{2,1,0:T(1,128)} %reshape.398.q_ref, s32[12,1,512]{2,1,0:T(1,128)} %reshape.400.k_ref, ...), custom_call_target="tpu_custom_call" | custom-call | flops 1000000000 | bytes 1000000 | tf_op jit(solution)/shard_map/prepare/pallas_call | solution.py:126
  71.5 9.9 %all-gather.8.cloned.1.call-done.x_ref = bf16[4096,768]{1,0:T(8,128)(2,1)} async-done(((bf16[512,768]{1,0:T(8,128)(2,1)}), bf16[4096,768]{1,0:T(8,128)(2,1)}) %all-gather.8.cloned.1.call-update) | async-done | bytes 6291472 | tf_op jit(solution)/shard_map/all_gather | solution.py:840
  81.5 9.5 %project.1 = (bf16[2,1024,256]{2,1,0:T(8,128)(2,1)}, bf16[2,2048,256]{2,1,0:T(8,128)(2,1)}) custom-call(bf16[4096,768]{1,0:T(8,128)(2,1)} %all-gather.8.cloned.1.call-done.x_ref, bf16[768,384]{1,0:T(8,128)(2,1)} %concatenate.36.w_ref, f32[1,384]{1,0:T(1,128)} %broadcast_in_dim.100.b_ref), custom_call_target="tpu_custom_call" | custom-call | flops 1000000000 | bytes 1000000 | tf_op jit(solution)/shard_map/project/pallas_call | solution.py:164
  91.0 42.4 %attend.1 = (bf16[12,512,128]{2,1,0:T(8,128)(2,1)}, bf16[12,512,128]{2,1,0:T(8,128)(2,1)}, f32[12,512,1]{2,1,0:T(8,128)}, f32[12,8,128]{2,1,0:T(8,128)}, bf16[8,256,256]{2,1,0:T(8,128)(2,1)}) custom-call(s32[12,512,1]{2,1,0:T(8,128)} %get-tuple-element.118.pq_ref, s32[12,512,1]{2,1,0:T(8,128)} %get-tuple-element.119.pk_ref, ...), custom_call_target="tpu_custom_call" | custom-call | flops 1000000000 | bytes 1000000 | tf_op jit(solution)/shard_map/attend/pallas_call | solution.py:284
  133.3 24.3 %all_to_all.41.got_ref = bf16[8,256,256]{2,1,0:T(8,128)(2,1)} all-to-all(bf16[8,256,256]{2,1,0:T(8,128)(2,1)} %get-tuple-element.129), channel_id=1, replica_groups=mesh['sq'=4,'own'=2,'hx'=2,'hc'=2] {'own','hx','hc'}, dimensions={0} | all-to-all | bytes 2097152 | tf_op jit(solution)/shard_map/all_to_all | solution.py:914
  157.7 47.0 %middle.1 = (bf16[512,768]{1,0:T(8,128)(2,1)}, bf16[8,128,256]{2,1,0:T(8,128)(2,1)}, bf16[8,128,256]{2,1,0:T(8,128)(2,1)}, f32[512,768]{1,0:T(8,128)}, bf16[2,76...) custom-call(s32[1]{0:T(128)} %bitcast.26.hc_ref, ...), custom_call_target="tpu_custom_call" | custom-call | flops 1000000000 | bytes 1000000 | tf_op jit(solution)/shard_map/middle/pallas_call | solution.py:721
  206.1 4.2 %all-to-all-start.3 = ((bf16[8,128,256]{2,1,0:T(8,128)(2,1)}), bf16[8,128,256]{2,1,0:T(8,128)(2,1)}, u32[]{:S(2)}, u32[]{:S(2)}) async-start(bf16[8,128,256]{2,1,0:T(8,128)(2,1)} %get-tuple-element.136), calls=%async_computation.3 | async-start | bytes 1048576 | tf_op jit(solution)/shard_map/all_to_all | solution.py:960
  220.2 2.9 fusion.2
  226.6 3.5 all-to-all-start.4
  235.5 28.0 %attend_back.2.full_ref = bf16[8,384,256]{2,1,0:T(8,128)(2,1)} custom-call(s32[12,512,1]{2,1,0:T(8,128)} %get-tuple-element.118.pq_ref, s32[12,512,1]{2,1,0:T(8,128)} %get-tuple-element.119.pk_ref, s32[12,1,512]{2,1,0:T(1,128)} %get-tuple-element.120.pqr_ref, s32[12,1,512]{2,1,0:T(1,128)} %get-tuple-element.121.pkr_ref, bf16[1024,256]{1,0:T(8,128)(2,1)} %bitcast.42.td_ref, ...), custom_call_target="tpu_custom_call" | custom-call | flops 1000000000 | bytes 1000000 | tf_op jit(solution)/shard_map/attend_back/pallas_call | solution.py:358
  264.4 4.1 %all-to-all-start.5 = ((bf16[8,384,256]{2,1,0:T(8,128)(2,1)}), bf16[8,384,256]{2,1,0:T(8,128)(2,1)S(1)}, u32[]{:S(2)}, u32[]{:S(2)}) async-start(bf16[8,384,256]{2,1,0:T(8,128)(2,1)} %attend_back.2.full_ref), calls=%async_computation.5 | async-start | bytes 3145728 | tf_op jit(solution)/shard_map/all_to_all | solution.py:996
  271.0 2.8 fusion.7
  280.7 15.6 %attend_back.3.half_ref = bf16[8,384,256]{2,1,0:T(8,128)(2,1)} custom-call(s32[12,512,1]{2,1,0:T(8,128)} %get-tuple-element.118.pq_ref, s32[12,512,1]{2,1,0:T(8,128)} %get-tuple-element.119.pk_ref, s32[12,1,512]{2,1,0:T(1,128)} %get-tuple-element.120.pqr_ref, s32[12,1,512]{2,1,0:T(1,128)} %get-tuple-element.121.pkr_ref, bf16[1024,256]{1,0:T(8,128)(2,1)} %bitcast.148, ...), custom_call_target="tpu_custom_call" | custom-call | flops 1000000000 | bytes 1000000 | tf_op jit(solution)/shard_map/attend_back/pallas_call | solution.py:358
  298.9 3.6 all-to-all-start.6
  311.3 9.9 %project_grad.1 = (bf16[768,384]{1,0:T(8,128)(2,1)}, f32[1,384]{1,0:T(1,128)}) custom-call(bf16[4096,768]{1,0:T(8,128)(2,1)} %all-gather.8.cloned.1.call-done.x_ref, bf16[8,384,256]{2,1,0:T(8,128)(2,1)} %attend_back.2.full_ref, bf16[8,384,256]{2,1,0:T(8,128)(2,1)} %attend_back.3.half_ref), custom_call_target="tpu_custom_call" | custom-call | flops 1000000000 | bytes 1000000 | tf_op jit(solution)/shard_map/project_grad/pallas_call | solution.py:417
  324.8 5.2 %collective-permute-done.10 = bf16[4,96,384]{2,1,0:T(8,128)(2,1)S(1)} collective-permute-done((bf16[4,96,384]{2,1,0:T(8,128)(2,1)S(1)}, bf16[4,96,384]{2,1,0:T(8,128)(2,1)S(1)}, u32[]{:S(2)}, u32[]{:S(2)}) %collective-permute-start.10) | collective-permute-done | bytes 294944 | tf_op jit(solution)/shard_map/ppermute | solution.py:785
  332.2 7.5 %project_back.1 = bf16[512,768]{1,0:T(8,128)(2,1)} custom-call(bf16[8,384,256]{2,1,0:T(8,128)(2,1)} %copy-done.2, bf16[8,384,256]{2,1,0:T(8,128)(2,1)} %copy-done.3, bf16[4,576,768]{2,1,0:T(8,128)(2,1)} %bitcast.142, f32[512,768]{1,0:T(8,128)} %get-tuple-element.183.dfi_ref), custom_call_target="tpu_custom_call" | custom-call | flops 1000000000 | bytes 1000000 | tf_op jit(solution)/shard_map/project_back/pallas_call | solution.py:462
  339.7 4.2 %all-to-all-start.7 = ((bf16[4,128,768]{2,1,0:T(8,128)(2,1)}), bf16[4,128,768]{2,1,0:T(8,128)(2,1)}, u32[]{:S(2)}, u32[]{:S(2)}) async-start(bf16[4,128,768]{2,1,0:T(8,128)(2,1)} %bitcast.144), calls=%async_computation.7 | async-start | bytes 1572864 | tf_op jit(solution)/shard_map/all_to_all | solution.py:1042
  358.1 8.3 %collective-permute-done.17 = f32[9216]{0:T(1024)S(1)} collective-permute-done((f32[9216]{0:T(1024)S(1)}, f32[9216]{0:T(1024)S(1)}, u32[]{:S(2)}, u32[]{:S(2)}) %collective-permute-start.17) | collective-permute-done | bytes 36896 | tf_op jit(solution)/shard_map/ppermute | solution.py:785
  366.4 4.5 %collective-permute-start.18 = (f32[9216]{0:T(1024)S(1)}, f32[9216]{0:T(1024)S(1)}, u32[]{:S(2)}, u32[]{:S(2)}) collective-permute-start(f32[9216]{0:T(1024)S(1)} %add.263), channel_id=1, source_target_pairs={{0,16},{8,24},{16,0},{24,8},{1,17},{9,25},{17,1},{25,9},{2,18},{10... | collective-permute-start | bytes 110600 | tf_op jit(solution)/shard_map/ppermute | solution.py:785
  371.0 3.1 collective-permute-done.12
  (210 shorter events, 90.6 us)
Async XLA Ops:
  7.2 29.5 %all-gather.10.cloned.1.call-start = ((), (), s32[]{:S(2)}) async-start(), calls=%async_computation.9 | async-start | bytes 1966080 | tf_op jit(solution)/shard_map/all_gather | solution.py:836
  10.0 71.4 %all-gather.8.cloned.1.call-start = ((), (), s32[]{:S(2)}) async-start(), calls=%async_computation.8 | async-start | bytes 7077888 | tf_op jit(solution)/shard_map/all_gather | solution.py:840
  46.9 24.6 %all-to-all-start.1 = ((bf16[4,128,768]{2,1,0:T(8,128)(2,1)}), bf16[4,128,768]{2,1,0:T(8,128)(2,1)S(1)}, u32[]{:S(2)}, u32[]{:S(2)}) async-start(bf16[4,128,768]{2,1,0:T(8,128)(2,1)} %param.24), calls=%async_computation.1 | async-start | bytes 1572864 | tf_op jit(solution)/shard_map/all_to_all | solution.py:841
  50.4 107.2 %all-gather.12.cloned.1.call-start = ((), (), s32[]{:S(2)}) async-start(), calls=%async_computation.10 | async-start | bytes 11796480 | tf_op jit(solution)/shard_map/all_gather | solution.py:910
  81.4 141.7 %all-gather.14.cloned.1.call-start = ((), (), s32[]{:S(2)}) async-start(), calls=%async_computation.11 | async-start | bytes 4423680 | tf_op jit(solution)/shard_map/all_gather | solution.py:918
  205.5 17.6 %collective-permute-start = (f32[16]{0:T(128)S(1)}, f32[16]{0:T(128)S(1)}, u32[]{:S(2)}, u32[]{:S(2)}) collective-permute-start(f32[16]{0:T(128)S(1)} %broadcast_select_fusion.3), channel_id=1, source_target_pairs={{0,4},{4,0},{1,5},{5,1},{2,6},{6,2},{3,7},{7,3},{8,12},{12,8},{9,1... | collective-permute-start | bytes 200 | tf_op jit(solution)/shard_map/ppermute | solution.py:785
  206.1 17.0 %all-to-all-start.3 = ((bf16[8,128,256]{2,1,0:T(8,128)(2,1)}), bf16[8,128,256]{2,1,0:T(8,128)(2,1)}, u32[]{:S(2)}, u32[]{:S(2)}) async-start(bf16[8,128,256]{2,1,0:T(8,128)(2,1)} %get-tuple-element.136), calls=%async_computation.3 | async-start | bytes 1048576 | tf_op jit(solution)/shard_map/all_to_all | solution.py:960
  223.1 40.4 %collective-permute-start.3 = (bf16[4,2,96,896]{3,2,0,1:T(8,128)(2,1)}, bf16[4,2,96,896]{3,2,0,1:T(8,128)(2,1)}, u32[]{:S(2)}, u32[]{:S(2)}) collective-permute-start(bf16[4,2,96,896]{3,2,0,1:T(8,128)(2,1)} %fusion), channel_id=1, source_target_pairs={{0,2},{2,0},{1,3},{3,1},{4,6},{6,4},{5,7},{7,5},{8,10},{10,8},{9,1... | collective-permute-start | bytes 4128776 | tf_op jit(solution)/shard_map/ppermute | solution.py:785
  225.1 38.5 %collective-permute-start.4 = (bf16[2,4,96,896]{3,2,1,0:T(8,128)(2,1)}, bf16[2,4,96,896]{3,2,1,0:T(8,128)(2,1)}, u32[]{:S(2)}, u32[]{:S(2)}) collective-permute-start(bf16[2,4,96,896]{3,2,1,0:T(8,128)(2,1)} %fusion.2), channel_id=1, source_target_pairs={{0,4},{4,0},{1,5},{5,1},{2,6},{6,2},{3,7},{7,3},{8,12},{12,8},{9,1... | collective-permute-start | bytes 4128776 | tf_op jit(solution)/shard_map/ppermute | solution.py:785
  226.6 36.9 %all-to-all-start.4 = ((bf16[8,128,256]{2,1,0:T(8,128)(2,1)}), bf16[8,128,256]{2,1,0:T(8,128)(2,1)S(1)}, u32[]{:S(2)}, u32[]{:S(2)}) async-start(bf16[8,128,256]{2,1,0:T(8,128)(2,1)} %get-tuple-element.149), calls=%async_computation.4 | async-start | bytes 1048576 | tf_op jit(solution)/shard_map/all_to_all | solution.py:989
  230.1 33.4 %collective-permute-start.5 = (bf16[128,768]{1,0:T(8,128)(2,1)S(1)}, bf16[128,768]{1,0:T(8,128)(2,1)S(1)}, u32[]{:S(2)}, u32[]{:S(2)}) collective-permute-start(bf16[128,768]{1,0:T(8,128)(2,1)S(1)} %copy-done.20), channel_id=1, source_target_pairs={{0,8},{8,16},{16,24},{24,0},{1,9},{9,17},{17,25},{25,1},{2,10},{10... | collective-permute-start | bytes 589832 | tf_op jit(solution)/shard_map/ppermute | solution.py:947
  231.6 31.9 %collective-permute-start.6 = (bf16[128,768]{1,0:T(8,128)(2,1)S(1)}, bf16[128,768]{1,0:T(8,128)(2,1)S(1)}, u32[]{:S(2)}, u32[]{:S(2)}) collective-permute-start(bf16[128,768]{1,0:T(8,128)(2,1)S(1)} %get-tuple-element.154), channel_id=1, source_target_pairs={{0,16},{8,24},{16,0},{24,8},{1,17},{9,25},{17,1},{25,9},{2,18},{10... | collective-permute-start | bytes 589832 | tf_op jit(solution)/shard_map/ppermute | solution.py:947
  234.0 29.5 %collective-permute-start.7 = (bf16[128,768]{1,0:T(8,128)(2,1)S(1)}, bf16[128,768]{1,0:T(8,128)(2,1)S(1)}, u32[]{:S(2)}, u32[]{:S(2)}) collective-permute-start(bf16[128,768]{1,0:T(8,128)(2,1)S(1)} %get-tuple-element.155), channel_id=1, source_target_pairs={{0,24},{8,0},{16,8},{24,16},{1,25},{9,1},{17,9},{25,17},{2,26},{10... | collective-permute-start | bytes 589832 | tf_op jit(solution)/shard_map/ppermute | solution.py:947
  264.4 33.3 %all-to-all-start.5 = ((bf16[8,384,256]{2,1,0:T(8,128)(2,1)}), bf16[8,384,256]{2,1,0:T(8,128)(2,1)S(1)}, u32[]{:S(2)}, u32[]{:S(2)}) async-start(bf16[8,384,256]{2,1,0:T(8,128)(2,1)} %attend_back.2.full_ref), calls=%async_computation.5 | async-start | bytes 3145728 | tf_op jit(solution)/shard_map/all_to_all | solution.py:996
  276.6 26.8 %collective-permute-start.8 = (bf16[4,96,896]{2,1,0:T(8,128)(2,1)}, bf16[4,96,896]{2,1,0:T(8,128)(2,1)}, u32[]{:S(2)}, u32[]{:S(2)}) collective-permute-start(bf16[4,96,896]{2,1,0:T(8,128)(2,1)} %get-tuple-element.169), channel_id=1, source_target_pairs={{0,4},{4,0},{1,5},{5,1},{2,6},{6,2},{3,7},{7,3},{8,12},{12,8},{9,1... | collective-permute-start | bytes 2064392 | tf_op jit(solution)/shard_map/ppermute | solution.py:785
  278.6 24.8 %collective-permute-start.9 = (bf16[4,96,896]{2,1,0:T(8,128)(2,1)}, bf16[4,96,896]{2,1,0:T(8,128)(2,1)}, u32[]{:S(2)}, u32[]{:S(2)}) collective-permute-start(bf16[4,96,896]{2,1,0:T(8,128)(2,1)} %get-tuple-element.170), channel_id=1, source_target_pairs={{0,2},{2,0},{1,3},{3,1},{4,6},{6,4},{5,7},{7,5},{8,10},{10,8},{9,1... | collective-permute-start | bytes 2064392 | tf_op jit(solution)/shard_map/ppermute | solution.py:785
  298.9 31.2 %all-to-all-start.6 = ((bf16[8,384,256]{2,1,0:T(8,128)(2,1)}), bf16[8,384,256]{2,1,0:T(8,128)(2,1)S(1)}, u32[]{:S(2)}, u32[]{:S(2)}) async-start(bf16[8,384,256]{2,1,0:T(8,128)(2,1)} %attend_back.3.half_ref), calls=%async_computation.6 | async-start | bytes 3145728 | tf_op jit(solution)/shard_map/all_to_all | solution.py:1007
  307.2 36.7 %collective-permute-start.19 = (bf16[96,1792]{1,0:T(8,128)(2,1)}, bf16[96,1792]{1,0:T(8,128)(2,1)}, u32[]{:S(2)}, u32[]{:S(2)}) collective-permute-start(bf16[96,1792]{1,0:T(8,128)(2,1)} %get-tuple-element.194), channel_id=1, source_target_pairs={{0,8},{8,16},{16,24},{24,0},{1,9},{9,17},{17,25},{25,1},{2,10},{10... | collective-permute-start | bytes 1032200 | tf_op jit(solution)/shard_map/ppermute | solution.py:947
  307.9 36.1 %collective-permute-start.20 = (bf16[96,1792]{1,0:T(8,128)(2,1)}, bf16[96,1792]{1,0:T(8,128)(2,1)}, u32[]{:S(2)}, u32[]{:S(2)}) collective-permute-start(bf16[96,1792]{1,0:T(8,128)(2,1)} %get-tuple-element.195), channel_id=1, source_target_pairs={{0,16},{8,24},{16,0},{24,8},{1,17},{9,25},{17,1},{25,9},{2,18},{10... | collective-permute-start | bytes 1032200 | tf_op jit(solution)/shard_map/ppermute | solution.py:947
  309.8 34.1 %collective-permute-start.21 = (bf16[96,1792]{1,0:T(8,128)(2,1)}, bf16[96,1792]{1,0:T(8,128)(2,1)}, u32[]{:S(2)}, u32[]{:S(2)}) collective-permute-start(bf16[96,1792]{1,0:T(8,128)(2,1)} %get-tuple-element.196), channel_id=1, source_target_pairs={{0,24},{8,0},{16,8},{24,16},{1,25},{9,1},{17,9},{25,17},{2,26},{10... | collective-permute-start | bytes 1032200 | tf_op jit(solution)/shard_map/ppermute | solution.py:947
  339.7 40.4 %all-to-all-start.7 = ((bf16[4,128,768]{2,1,0:T(8,128)(2,1)}), bf16[4,128,768]{2,1,0:T(8,128)(2,1)}, u32[]{:S(2)}, u32[]{:S(2)}) async-start(bf16[4,128,768]{2,1,0:T(8,128)(2,1)} %bitcast.144), calls=%async_computation.7 | async-start | bytes 1572864 | tf_op jit(solution)/shard_map/all_to_all | solution.py:1042
  350.9 20.1 %collective-permute-start.11 = (bf16[96,576]{1,0:T(8,128)(2,1)S(1)}, bf16[96,576]{1,0:T(8,128)(2,1)S(1)}, u32[]{:S(2)}, u32[]{:S(2)}) collective-permute-start(bf16[96,576]{1,0:T(8,128)(2,1)S(1)} %get-tuple-element.189), channel_id=1, source_target_pairs={{0,8},{8,16},{16,24},{24,0},{1,9},{9,17},{17,25},{25,1},{2,10},{10... | collective-permute-start | bytes 331784 | tf_op jit(solution)/shard_map/ppermute | solution.py:947
  352.9 21.2 %collective-permute-start.12 = (bf16[96,576]{1,0:T(8,128)(2,1)S(1)}, bf16[96,576]{1,0:T(8,128)(2,1)S(1)}, u32[]{:S(2)}, u32[]{:S(2)}) collective-permute-start(bf16[96,576]{1,0:T(8,128)(2,1)S(1)} %get-tuple-element.190), channel_id=1, source_target_pairs={{0,16},{8,24},{16,0},{24,8},{1,17},{9,25},{17,1},{25,9},{2,18},{10... | collective-permute-start | bytes 331784 | tf_op jit(solution)/shard_map/ppermute | solution.py:947
  355.3 18.8 %collective-permute-start.13 = (bf16[96,576]{1,0:T(8,128)(2,1)S(1)}, bf16[96,576]{1,0:T(8,128)(2,1)S(1)}, u32[]{:S(2)}, u32[]{:S(2)}) collective-permute-start(bf16[96,576]{1,0:T(8,128)(2,1)S(1)} %get-tuple-element.191), channel_id=1, source_target_pairs={{0,24},{8,0},{16,8},{24,16},{1,25},{9,1},{17,9},{25,17},{2,26},{10... | collective-permute-start | bytes 331784 | tf_op jit(solution)/shard_map/ppermute | solution.py:947
  (38 other events, 415.9 us)
Sparse Core Ops, SparseCore 0:
  10.1 22.3 all-gather.9
  36.8 44.5 all-gather.7
  82.9 69.0 all-gather.11
  157.8 29.8 all-gather.13
where the time goes:
time: 391 us; the launch traced here: 389 us
  Pallas kernels  171 us (44%)
  starting transfers between devices  56.6 us (14%)
  blocking collectives  50.8 us (13%)
  local copies, waits for them, and re-layouts  33.3 us (9%)
  other arithmetic  32.7 us (8%)
  waiting for transfers between devices  30.8 us (8%)
  between operations  14.4 us (4%)
    pallas_call x1, Pallas kernels, middle(): pl.pallas_call(functools.partial(middle_body, heads), grid_spec=pltpu.Pre...  47 us
    pallas_call x2, Pallas kernels, attend_back(): pl.pallas_call(attend_back_body, grid=(steps,), in_specs=[col, col, line,...  43.6 us
    pallas_call x1, Pallas kernels, attend(): pl.pallas_call(attend_body, grid=(STEPS,), in_specs=[chunk(1), chunk(1),...  42.4 us
    all_to_all x1, blocking collectives, per_device(): x_own = lax.all_to_all(mine, 'sq', 0, 0, tiled=True).reshape(tokens, width)  26.5 us
    all_to_all x1, blocking collectives, per_device(): got = lax.all_to_all(done, PLANE, 0, 0, tiled=True)  24.3 us
    ppermute x13, starting transfers between devices, swap(): return lax.ppermute(x, axis, [(i, i ^ bit) for i in range(size)])  18.2 us
    ppermute x13, waiting for transfers between devices, swap(): return lax.ppermute(x, axis, [(i, i ^ bit) for i in range(size)])  17.7 us
    convert_element_type x9, other arithmetic, plus(): return (a.astype(F32) + b.astype(F32)).astype(BF)  17.1 us
  transfers between devices with their start and end apart: 32, of which 8 were waited for; matrix products, arithmetic and copies ran while one was open for 15% of the time, Pallas kernels for 44%

commit v1 on v0

--- a/solution.py
+++ b/solution.py
@@ -475,14 +475,13 @@
 
 
 def erf_parts(u):
-    mag = jnp.abs(u) * (0.5**0.5)
-    bell = jnp.exp(-(mag * mag))
-    t = 1.0 / (1.0 + 0.3275911 * mag)
+    bell = jnp.exp2(u * u * (-0.5 * 1.4426950408889634))
+    t = 1.0 / (1.0 + (0.3275911 * 0.5**0.5) * jnp.abs(u))
     poly = t * (
-        0.254829592
-        + t * (-0.284496736 + t * (1.421413741 + t * (-1.453152027 + t * 1.061405429)))
-    )
-    tail = 0.5 * poly * bell
+        0.127414796
+        + t * (-0.142248368 + t * (0.7107068705 + t * (-0.7265760135 + t * 0.5307027145)))
+    )
+    tail = poly * bell
     return jnp.where(u < 0, tail, 1.0 - tail), bell * ((2 * jnp.pi) ** -0.5)
 
 
@@ -529,11 +528,22 @@
     dlow_t_ref,
     dup_ref,
     rows_back_ref,
+    down_buf,
+    up_buf,
+    side_buf,
+    main_sems,
+    side_sems,
 ):
     step = pl.program_id(0)
     tokens, width = x_ref.shape
     hid = up_ref.shape[2]
     size = 64
+
+    def main_copies(c, k, down_to, up_to):
+        return [
+            pltpu.make_async_copy(buf.at[c], to.at[k, :, pl.ds(0, hid)], main_sems.at[c, i])
+            for i, (buf, to) in enumerate(((down_buf, down_to), (up_buf, up_to)))
+        ]
 
     def tiles(body, carry):
         def at(i, carry):
@@ -587,7 +597,8 @@
             hid_ref[step, :, cols] = (u * phi).astype(BF)
             slope_ref[step, :, cols] = phi + u * bell
 
-        columns(hid, upper)
+        for n in range(0, hid, 256):
+            upper(slice(n, n + 256))
         acc_ref[...] += nn(hid_ref[step], down_ref[0])
 
     @pl.when(step == heads)
@@ -625,18 +636,21 @@
 
         acc_ref[...] += nt(dup_ref[...], up_ref[0])
 
-        for there, k, down_to, up_to in (
-            (c < heads // 2, c, down_sent_ref, up_sent_ref),
-            (c >= heads // 2, c - heads // 2, down_kept_ref, up_kept_ref),
-        ):
-
-            @pl.when(there)
-            def _():
-                def products(cols):
-                    down_to[k, :, cols] = nn(dlow_t_ref[...], hid_ref[c, :, cols]).astype(BF)
-                    up_to[k, :, cols] = nn(low_t_ref[...], dup_ref[:, cols]).astype(BF)
-
-                columns(hid, products)
+        def products(cols):
+            down_buf[c, :, cols] = nn(dlow_t_ref[...], hid_ref[c, :, cols]).astype(BF)
+            up_buf[c, :, cols] = nn(low_t_ref[...], dup_ref[:, cols]).astype(BF)
+
+        columns(hid, products)
+
+        @pl.when(c < heads // 2)
+        def _():
+            for copy in main_copies(c, c, down_sent_ref, up_sent_ref):
+                copy.start()
+
+        @pl.when(c >= heads // 2)
+        def _():
+            for copy in main_copies(c, c - heads // 2, down_kept_ref, up_kept_ref):
+                copy.start()
 
     @pl.when(step == 2 * heads - 1)
     def _():
@@ -682,19 +696,24 @@
             at = pl.multiple_of(chunk_at(k, heads, hc_ref[0]) * 256, 256)
             whole = nn(dlow_t_ref[...], rows_ref[:, pl.ds(at, 256)]).astype(BF)
 
-            @pl.when(k < heads // 2)
-            def _():
-                down_sent_ref[k, :, hid:] = whole[:, :SIDE]
-                up_sent_ref[k, :, hid:] = whole[:, SIDE:]
-
-            @pl.when(k >= heads // 2)
-            def _():
-                down_kept_ref[k - heads // 2, :, hid:] = whole[:, :SIDE]
-                up_kept_ref[k - heads // 2, :, hid:] = whole[:, SIDE:]
-
+            side_buf[k, 0] = whole[:, :SIDE]
+            side_buf[k, 1] = whole[:, SIDE:]
             return carry
 
         lax.fori_loop(0, heads, grad, 0)
+        copies = []
+        for k in range(heads):
+            pairs = heads // 2
+            to = (down_sent_ref, up_sent_ref) if k < pairs else (down_kept_ref, up_kept_ref)
+            copies += main_copies(k, k % pairs, *to)
+            for i in range(2):
+                side = pltpu.make_async_copy(
+                    side_buf.at[k, i], to[i].at[k % pairs, :, pl.ds(hid, SIDE)], side_sems.at[k, i]
+                )
+                side.start()
+                copies.append(side)
+        for copy in copies:
+            copy.wait()
 
 
 def chunk_at(k, heads, hc):
@@ -713,9 +732,7 @@
     once = lambda *shape: pl.BlockSpec(shape, lambda g, c: (0,) * len(shape))
     by_chunk = lambda part, *shape: pl.BlockSpec(shape, lambda g, c: (at(g % heads, c), part, 0))
     late = lambda *shape: pl.BlockSpec(shape, lambda g, c: (at(jnp.maximum(g - heads, 0), c), 0, 0))
-    grads = pl.BlockSpec(
-        (pairs, width, hid + SIDE), lambda g, c: (0, 0, 0), pipeline_mode=pl.Buffered(1)
-    )
+    grads = pl.BlockSpec(memory_space=pl.ANY)
     big = jax.ShapeDtypeStruct((pairs, width, hid + SIDE), BF)
     table = jax.ShapeDtypeStruct((OWN * heads, 128, 256), BF)
     return pl.pallas_call(
@@ -760,6 +777,11 @@
                 pltpu.VMEM((width, tokens), BF),
                 pltpu.VMEM((tokens, hid), BF),
                 pltpu.VMEM((tokens, heads * 256), BF),
+                pltpu.VMEM((heads, width, hid), BF),
+                pltpu.VMEM((heads, width, hid), BF),
+                pltpu.VMEM((heads, 2, width, SIDE), BF),
+                pltpu.SemaphoreType.DMA((heads, 2)),
+                pltpu.SemaphoreType.DMA((heads, 2)),
             ],
         ),
         out_shape=[

time: 391 us -> 387 us (0.990)
  Pallas kernels: 171 us -> 166 us
    pallas_call x1, Pallas kernels: 47 us -> 42.8 us  [middle(): pl.pallas_call(functools.partial(middle_body, heads), grid_spec=pltpu.Pre...]
  transfers between devices with their start and end apart: 32 -> 32, of which waited for: 8 -> 8; matrix products, arithmetic and copies ran while one was open for 15% -> 15% of each run, Pallas kernels for 44% -> 43%
where the time goes in v1:
time: 387 us; the launch traced here: 385 us
  Pallas kernels  166 us (43%)
  starting transfers between devices  56.6 us (15%)
  blocking collectives  50.8 us (13%)
  local copies, waits for them, and re-layouts  33.3 us (9%)
  other arithmetic  32.7 us (8%)
  waiting for transfers between devices  30.8 us (8%)
  between operations  14.4 us (4%)
    pallas_call x2, Pallas kernels, attend_back(): pl.pallas_call(attend_back_body, grid=(steps,), in_specs=[col, col, line,...  43.6 us
    pallas_call x1, Pallas kernels, middle(): pl.pallas_call(functools.partial(middle_body, heads), grid_spec=pltpu.Pre...  42.8 us
    pallas_call x1, Pallas kernels, attend(): pl.pallas_call(attend_body, grid=(STEPS,), in_specs=[chunk(1), chunk(1),...  42.4 us
    all_to_all x1, blocking collectives, per_device(): x_own = lax.all_to_all(mine, 'sq', 0, 0, tiled=True).reshape(tokens, width)  26.5 us
    all_to_all x1, blocking collectives, per_device(): got = lax.all_to_all(done, PLANE, 0, 0, tiled=True)  24.3 us
    ppermute x13, starting transfers between devices, swap(): return lax.ppermute(x, axis, [(i, i ^ bit) for i in range(size)])  18.2 us
    ppermute x13, waiting for transfers between devices, swap(): return lax.ppermute(x, axis, [(i, i ^ bit) for i in range(size)])  17.7 us
    convert_element_type x9, other arithmetic, plus(): return (a.astype(F32) + b.astype(F32)).astype(BF)  17.1 us
  transfers between devices with their start and end apart: 32, of which 8 were waited for; matrix products, arithmetic and copies ran while one was open for 15% of the time, Pallas kernels for 43%

profile of v1, /device:TPU:0, one launch (start us, length us, event | category | flops | bytes accessed | tf_op | source)
XLA Modules:
  0.0 384.8 jit_solution(14243761133689391545)
XLA Ops:
  10.2 26.5 %all_to_all.40 = bf16[4,128,768]{2,1,0:T(8,128)(2,1)} all-to-all(bf16[4,128,768]{2,1,0:T(8,128)(2,1)S(1)} %constant_dynamic-slice_fusion.7), channel_id=1, replica_groups=mesh['sq'=4,'own'=2,'hx'=2,'hc'=2] {'sq'}, dimensions={0} | all-to-all | bytes 1572864 | tf_op jit(solution)/shard_map/all_to_all | solution.py:857
  40.1 2.9 pad_maximum_fusion
  46.9 3.5 all-to-all-start.1
  54.0 10.7 %prepare.1 = (s32[12,512,1]{2,1,0:T(8,128)}, s32[12,512,1]{2,1,0:T(8,128)}, s32[12,1,512]{2,1,0:T(1,128)}, s32[12,1,512]{2,1,0:T(1,128)}, f32[512,1]{1,0:T(8,128)}, /*index=5*/s32[12,1,512]{2,1,0:T(1,128)}) custom-call(s32[2]{0:T(128)} %pad_add_fusion.2.here_ref, s32[12,1,512]{2,1,0:T(1,128)} %reshape.398.q_ref, s32[12,1,512]{2,1,0:T(1,128)} %reshape.400.k_ref, ...), custom_call_target="tpu_custom_call" | custom-call | flops 1000000000 | bytes 1000000 | tf_op jit(solution)/shard_map/prepare/pallas_call | solution.py:126
  71.5 9.9 %all-gather.8.cloned.1.call-done.x_ref = bf16[4096,768]{1,0:T(8,128)(2,1)} async-done(((bf16[512,768]{1,0:T(8,128)(2,1)}), bf16[4096,768]{1,0:T(8,128)(2,1)}) %all-gather.8.cloned.1.call-update) | async-done | bytes 6291472 | tf_op jit(solution)/shard_map/all_gather | solution.py:862
  81.5 9.5 %project.1 = (bf16[2,1024,256]{2,1,0:T(8,128)(2,1)}, bf16[2,2048,256]{2,1,0:T(8,128)(2,1)}) custom-call(bf16[4096,768]{1,0:T(8,128)(2,1)} %all-gather.8.cloned.1.call-done.x_ref, bf16[768,384]{1,0:T(8,128)(2,1)} %concatenate.36.w_ref, f32[1,384]{1,0:T(1,128)} %broadcast_in_dim.100.b_ref), custom_call_target="tpu_custom_call" | custom-call | flops 1000000000 | bytes 1000000 | tf_op jit(solution)/shard_map/project/pallas_call | solution.py:164
  91.0 42.4 %attend.1 = (bf16[12,512,128]{2,1,0:T(8,128)(2,1)}, bf16[12,512,128]{2,1,0:T(8,128)(2,1)}, f32[12,512,1]{2,1,0:T(8,128)}, f32[12,8,128]{2,1,0:T(8,128)}, bf16[8,256,256]{2,1,0:T(8,128)(2,1)}) custom-call(s32[12,512,1]{2,1,0:T(8,128)} %get-tuple-element.118.pq_ref, s32[12,512,1]{2,1,0:T(8,128)} %get-tuple-element.119.pk_ref, ...), custom_call_target="tpu_custom_call" | custom-call | flops 1000000000 | bytes 1000000 | tf_op jit(solution)/shard_map/attend/pallas_call | solution.py:284
  133.3 24.3 %all_to_all.41.got_ref = bf16[8,256,256]{2,1,0:T(8,128)(2,1)} all-to-all(bf16[8,256,256]{2,1,0:T(8,128)(2,1)} %get-tuple-element.129), channel_id=1, replica_groups=mesh['sq'=4,'own'=2,'hx'=2,'hc'=2] {'own','hx','hc'}, dimensions={0} | all-to-all | bytes 2097152 | tf_op jit(solution)/shard_map/all_to_all | solution.py:936
  157.7 42.8 %middle.1 = (bf16[512,768]{1,0:T(8,128)(2,1)}, bf16[8,128,256]{2,1,0:T(8,128)(2,1)}, bf16[8,128,256]{2,1,0:T(8,128)(2,1)}, f32[512,768]{1,0:T(8,128)}, bf16[2,76...) custom-call(s32[1]{0:T(128)} %bitcast.26.hc_ref, ...), custom_call_target="tpu_custom_call" | custom-call | flops 1000000000 | bytes 1000000 | tf_op jit(solution)/shard_map/middle/pallas_call | solution.py:738
  201.9 4.2 %all-to-all-start.3 = ((bf16[8,128,256]{2,1,0:T(8,128)(2,1)}), bf16[8,128,256]{2,1,0:T(8,128)(2,1)}, u32[]{:S(2)}, u32[]{:S(2)}) async-start(bf16[8,128,256]{2,1,0:T(8,128)(2,1)} %get-tuple-element.136), calls=%async_computation.3 | async-start | bytes 1048576 | tf_op jit(solution)/shard_map/all_to_all | solution.py:982
  216.0 2.9 fusion.2
  222.4 3.5 all-to-all-start.4
  231.3 28.0 %attend_back.2.full_ref = bf16[8,384,256]{2,1,0:T(8,128)(2,1)} custom-call(s32[12,512,1]{2,1,0:T(8,128)} %get-tuple-element.118.pq_ref, s32[12,512,1]{2,1,0:T(8,128)} %get-tuple-element.119.pk_ref, s32[12,1,512]{2,1,0:T(1,128)} %get-tuple-element.120.pqr_ref, s32[12,1,512]{2,1,0:T(1,128)} %get-tuple-element.121.pkr_ref, bf16[1024,256]{1,0:T(8,128)(2,1)} %bitcast.42.td_ref, ...), custom_call_target="tpu_custom_call" | custom-call | flops 1000000000 | bytes 1000000 | tf_op jit(solution)/shard_map/attend_back/pallas_call | solution.py:358
  260.2 4.1 %all-to-all-start.5 = ((bf16[8,384,256]{2,1,0:T(8,128)(2,1)}), bf16[8,384,256]{2,1,0:T(8,128)(2,1)S(1)}, u32[]{:S(2)}, u32[]{:S(2)}) async-start(bf16[8,384,256]{2,1,0:T(8,128)(2,1)} %attend_back.2.full_ref), calls=%async_computation.5 | async-start | bytes 3145728 | tf_op jit(solution)/shard_map/all_to_all | solution.py:1018
  266.8 2.8 fusion.7
  276.5 15.6 %attend_back.3.half_ref = bf16[8,384,256]{2,1,0:T(8,128)(2,1)} custom-call(s32[12,512,1]{2,1,0:T(8,128)} %get-tuple-element.118.pq_ref, s32[12,512,1]{2,1,0:T(8,128)} %get-tuple-element.119.pk_ref, s32[12,1,512]{2,1,0:T(1,128)} %get-tuple-element.120.pqr_ref, s32[12,1,512]{2,1,0:T(1,128)} %get-tuple-element.121.pkr_ref, bf16[1024,256]{1,0:T(8,128)(2,1)} %bitcast.148, ...), custom_call_target="tpu_custom_call" | custom-call | flops 1000000000 | bytes 1000000 | tf_op jit(solution)/shard_map/attend_back/pallas_call | solution.py:358
  294.6 3.6 all-to-all-start.6
  307.1 9.9 %project_grad.1 = (bf16[768,384]{1,0:T(8,128)(2,1)}, f32[1,384]{1,0:T(1,128)}) custom-call(bf16[4096,768]{1,0:T(8,128)(2,1)} %all-gather.8.cloned.1.call-done.x_ref, bf16[8,384,256]{2,1,0:T(8,128)(2,1)} %attend_back.2.full_ref, bf16[8,384,256]{2,1,0:T(8,128)(2,1)} %attend_back.3.half_ref), custom_call_target="tpu_custom_call" | custom-call | flops 1000000000 | bytes 1000000 | tf_op jit(solution)/shard_map/project_grad/pallas_call | solution.py:417
  320.6 5.2 %collective-permute-done.10 = bf16[4,96,384]{2,1,0:T(8,128)(2,1)S(1)} collective-permute-done((bf16[4,96,384]{2,1,0:T(8,128)(2,1)S(1)}, bf16[4,96,384]{2,1,0:T(8,128)(2,1)S(1)}, u32[]{:S(2)}, u32[]{:S(2)}) %collective-permute-start.10) | collective-permute-done | bytes 294944 | tf_op jit(solution)/shard_map/ppermute | solution.py:807
  328.0 7.5 %project_back.1 = bf16[512,768]{1,0:T(8,128)(2,1)} custom-call(bf16[8,384,256]{2,1,0:T(8,128)(2,1)} %copy-done.2, bf16[8,384,256]{2,1,0:T(8,128)(2,1)} %copy-done.3, bf16[4,576,768]{2,1,0:T(8,128)(2,1)} %bitcast.142, f32[512,768]{1,0:T(8,128)} %get-tuple-element.183.dfi_ref), custom_call_target="tpu_custom_call" | custom-call | flops 1000000000 | bytes 1000000 | tf_op jit(solution)/shard_map/project_back/pallas_call | solution.py:462
  335.5 4.2 %all-to-all-start.7 = ((bf16[4,128,768]{2,1,0:T(8,128)(2,1)}), bf16[4,128,768]{2,1,0:T(8,128)(2,1)}, u32[]{:S(2)}, u32[]{:S(2)}) async-start(bf16[4,128,768]{2,1,0:T(8,128)(2,1)} %bitcast.144), calls=%async_computation.7 | async-start | bytes 1572864 | tf_op jit(solution)/shard_map/all_to_all | solution.py:1064
  353.9 8.3 %collective-permute-done.17 = f32[9216]{0:T(1024)S(1)} collective-permute-done((f32[9216]{0:T(1024)S(1)}, f32[9216]{0:T(1024)S(1)}, u32[]{:S(2)}, u32[]{:S(2)}) %collective-permute-start.17) | collective-permute-done | bytes 36896 | tf_op jit(solution)/shard_map/ppermute | solution.py:807
  362.2 4.5 %collective-permute-start.18 = (f32[9216]{0:T(1024)S(1)}, f32[9216]{0:T(1024)S(1)}, u32[]{:S(2)}, u32[]{:S(2)}) collective-permute-start(f32[9216]{0:T(1024)S(1)} %add.263), channel_id=1, source_target_pairs={{0,16},{8,24},{16,0},{24,8},{1,17},{9,25},{17,1},{25,9},{2,18},{10... | collective-permute-start | bytes 110600 | tf_op jit(solution)/shard_map/ppermute | solution.py:807
  366.8 3.1 collective-permute-done.12
  (210 shorter events, 90.6 us)
Async XLA Ops:
  7.2 29.5 %all-gather.10.cloned.1.call-start = ((), (), s32[]{:S(2)}) async-start(), calls=%async_computation.9 | async-start | bytes 1966080 | tf_op jit(solution)/shard_map/all_gather | solution.py:858
  10.0 71.4 %all-gather.8.cloned.1.call-start = ((), (), s32[]{:S(2)}) async-start(), calls=%async_computation.8 | async-start | bytes 7077888 | tf_op jit(solution)/shard_map/all_gather | solution.py:862
  46.9 24.6 %all-to-all-start.1 = ((bf16[4,128,768]{2,1,0:T(8,128)(2,1)}), bf16[4,128,768]{2,1,0:T(8,128)(2,1)S(1)}, u32[]{:S(2)}, u32[]{:S(2)}) async-start(bf16[4,128,768]{2,1,0:T(8,128)(2,1)} %param.24), calls=%async_computation.1 | async-start | bytes 1572864 | tf_op jit(solution)/shard_map/all_to_all | solution.py:863
  50.4 107.2 %all-gather.12.cloned.1.call-start = ((), (), s32[]{:S(2)}) async-start(), calls=%async_computation.10 | async-start | bytes 11796480 | tf_op jit(solution)/shard_map/all_gather | solution.py:932
  81.4 137.5 %all-gather.14.cloned.1.call-start = ((), (), s32[]{:S(2)}) async-start(), calls=%async_computation.11 | async-start | bytes 4423680 | tf_op jit(solution)/shard_map/all_gather | solution.py:940
  201.3 17.6 %collective-permute-start = (f32[16]{0:T(128)S(1)}, f32[16]{0:T(128)S(1)}, u32[]{:S(2)}, u32[]{:S(2)}) collective-permute-start(f32[16]{0:T(128)S(1)} %broadcast_select_fusion.3), channel_id=1, source_target_pairs={{0,4},{4,0},{1,5},{5,1},{2,6},{6,2},{3,7},{7,3},{8,12},{12,8},{9,1... | collective-permute-start | bytes 200 | tf_op jit(solution)/shard_map/ppermute | solution.py:807
  201.9 17.0 %all-to-all-start.3 = ((bf16[8,128,256]{2,1,0:T(8,128)(2,1)}), bf16[8,128,256]{2,1,0:T(8,128)(2,1)}, u32[]{:S(2)}, u32[]{:S(2)}) async-start(bf16[8,128,256]{2,1,0:T(8,128)(2,1)} %get-tuple-element.136), calls=%async_computation.3 | async-start | bytes 1048576 | tf_op jit(solution)/shard_map/all_to_all | solution.py:982
  218.9 40.4 %collective-permute-start.3 = (bf16[4,2,96,896]{3,2,0,1:T(8,128)(2,1)}, bf16[4,2,96,896]{3,2,0,1:T(8,128)(2,1)}, u32[]{:S(2)}, u32[]{:S(2)}) collective-permute-start(bf16[4,2,96,896]{3,2,0,1:T(8,128)(2,1)} %fusion), channel_id=1, source_target_pairs={{0,2},{2,0},{1,3},{3,1},{4,6},{6,4},{5,7},{7,5},{8,10},{10,8},{9,1... | collective-permute-start | bytes 4128776 | tf_op jit(solution)/shard_map/ppermute | solution.py:807
  220.9 38.5 %collective-permute-start.4 = (bf16[2,4,96,896]{3,2,1,0:T(8,128)(2,1)}, bf16[2,4,96,896]{3,2,1,0:T(8,128)(2,1)}, u32[]{:S(2)}, u32[]{:S(2)}) collective-permute-start(bf16[2,4,96,896]{3,2,1,0:T(8,128)(2,1)} %fusion.2), channel_id=1, source_target_pairs={{0,4},{4,0},{1,5},{5,1},{2,6},{6,2},{3,7},{7,3},{8,12},{12,8},{9,1... | collective-permute-start | bytes 4128776 | tf_op jit(solution)/shard_map/ppermute | solution.py:807
  222.4 36.9 %all-to-all-start.4 = ((bf16[8,128,256]{2,1,0:T(8,128)(2,1)}), bf16[8,128,256]{2,1,0:T(8,128)(2,1)S(1)}, u32[]{:S(2)}, u32[]{:S(2)}) async-start(bf16[8,128,256]{2,1,0:T(8,128)(2,1)} %get-tuple-element.149), calls=%async_computation.4 | async-start | bytes 1048576 | tf_op jit(solution)/shard_map/all_to_all | solution.py:1011
  225.9 33.4 %collective-permute-start.5 = (bf16[128,768]{1,0:T(8,128)(2,1)S(1)}, bf16[128,768]{1,0:T(8,128)(2,1)S(1)}, u32[]{:S(2)}, u32[]{:S(2)}) collective-permute-start(bf16[128,768]{1,0:T(8,128)(2,1)S(1)} %copy-done.20), channel_id=1, source_target_pairs={{0,8},{8,16},{16,24},{24,0},{1,9},{9,17},{17,25},{25,1},{2,10},{10... | collective-permute-start | bytes 589832 | tf_op jit(solution)/shard_map/ppermute | solution.py:969
  227.4 31.8 %collective-permute-start.6 = (bf16[128,768]{1,0:T(8,128)(2,1)S(1)}, bf16[128,768]{1,0:T(8,128)(2,1)S(1)}, u32[]{:S(2)}, u32[]{:S(2)}) collective-permute-start(bf16[128,768]{1,0:T(8,128)(2,1)S(1)} %get-tuple-element.154), channel_id=1, source_target_pairs={{0,16},{8,24},{16,0},{24,8},{1,17},{9,25},{17,1},{25,9},{2,18},{10... | collective-permute-start | bytes 589832 | tf_op jit(solution)/shard_map/ppermute | solution.py:969
  229.8 29.5 %collective-permute-start.7 = (bf16[128,768]{1,0:T(8,128)(2,1)S(1)}, bf16[128,768]{1,0:T(8,128)(2,1)S(1)}, u32[]{:S(2)}, u32[]{:S(2)}) collective-permute-start(bf16[128,768]{1,0:T(8,128)(2,1)S(1)} %get-tuple-element.155), channel_id=1, source_target_pairs={{0,24},{8,0},{16,8},{24,16},{1,25},{9,1},{17,9},{25,17},{2,26},{10... | collective-permute-start | bytes 589832 | tf_op jit(solution)/shard_map/ppermute | solution.py:969
  260.2 33.3 %all-to-all-start.5 = ((bf16[8,384,256]{2,1,0:T(8,128)(2,1)}), bf16[8,384,256]{2,1,0:T(8,128)(2,1)S(1)}, u32[]{:S(2)}, u32[]{:S(2)}) async-start(bf16[8,384,256]{2,1,0:T(8,128)(2,1)} %attend_back.2.full_ref), calls=%async_computation.5 | async-start | bytes 3145728 | tf_op jit(solution)/shard_map/all_to_all | solution.py:1018
  272.4 26.8 %collective-permute-start.8 = (bf16[4,96,896]{2,1,0:T(8,128)(2,1)}, bf16[4,96,896]{2,1,0:T(8,128)(2,1)}, u32[]{:S(2)}, u32[]{:S(2)}) collective-permute-start(bf16[4,96,896]{2,1,0:T(8,128)(2,1)} %get-tuple-element.169), channel_id=1, source_target_pairs={{0,4},{4,0},{1,5},{5,1},{2,6},{6,2},{3,7},{7,3},{8,12},{12,8},{9,1... | collective-permute-start | bytes 2064392 | tf_op jit(solution)/shard_map/ppermute | solution.py:807
  274.4 24.9 %collective-permute-start.9 = (bf16[4,96,896]{2,1,0:T(8,128)(2,1)}, bf16[4,96,896]{2,1,0:T(8,128)(2,1)}, u32[]{:S(2)}, u32[]{:S(2)}) collective-permute-start(bf16[4,96,896]{2,1,0:T(8,128)(2,1)} %get-tuple-element.170), channel_id=1, source_target_pairs={{0,2},{2,0},{1,3},{3,1},{4,6},{6,4},{5,7},{7,5},{8,10},{10,8},{9,1... | collective-permute-start | bytes 2064392 | tf_op jit(solution)/shard_map/ppermute | solution.py:807
  294.6 31.2 %all-to-all-start.6 = ((bf16[8,384,256]{2,1,0:T(8,128)(2,1)}), bf16[8,384,256]{2,1,0:T(8,128)(2,1)S(1)}, u32[]{:S(2)}, u32[]{:S(2)}) async-start(bf16[8,384,256]{2,1,0:T(8,128)(2,1)} %attend_back.3.half_ref), calls=%async_computation.6 | async-start | bytes 3145728 | tf_op jit(solution)/shard_map/all_to_all | solution.py:1029
  303.0 36.7 %collective-permute-start.19 = (bf16[96,1792]{1,0:T(8,128)(2,1)}, bf16[96,1792]{1,0:T(8,128)(2,1)}, u32[]{:S(2)}, u32[]{:S(2)}) collective-permute-start(bf16[96,1792]{1,0:T(8,128)(2,1)} %get-tuple-element.194), channel_id=1, source_target_pairs={{0,8},{8,16},{16,24},{24,0},{1,9},{9,17},{17,25},{25,1},{2,10},{10... | collective-permute-start | bytes 1032200 | tf_op jit(solution)/shard_map/ppermute | solution.py:969
  303.7 36.0 %collective-permute-start.20 = (bf16[96,1792]{1,0:T(8,128)(2,1)}, bf16[96,1792]{1,0:T(8,128)(2,1)}, u32[]{:S(2)}, u32[]{:S(2)}) collective-permute-start(bf16[96,1792]{1,0:T(8,128)(2,1)} %get-tuple-element.195), channel_id=1, source_target_pairs={{0,16},{8,24},{16,0},{24,8},{1,17},{9,25},{17,1},{25,9},{2,18},{10... | collective-permute-start | bytes 1032200 | tf_op jit(solution)/shard_map/ppermute | solution.py:969
  305.6 34.1 %collective-permute-start.21 = (bf16[96,1792]{1,0:T(8,128)(2,1)}, bf16[96,1792]{1,0:T(8,128)(2,1)}, u32[]{:S(2)}, u32[]{:S(2)}) collective-permute-start(bf16[96,1792]{1,0:T(8,128)(2,1)} %get-tuple-element.196), channel_id=1, source_target_pairs={{0,24},{8,0},{16,8},{24,16},{1,25},{9,1},{17,9},{25,17},{2,26},{10... | collective-permute-start | bytes 1032200 | tf_op jit(solution)/shard_map/ppermute | solution.py:969
  335.5 40.4 %all-to-all-start.7 = ((bf16[4,128,768]{2,1,0:T(8,128)(2,1)}), bf16[4,128,768]{2,1,0:T(8,128)(2,1)}, u32[]{:S(2)}, u32[]{:S(2)}) async-start(bf16[4,128,768]{2,1,0:T(8,128)(2,1)} %bitcast.144), calls=%async_computation.7 | async-start | bytes 1572864 | tf_op jit(solution)/shard_map/all_to_all | solution.py:1064
  346.7 20.1 %collective-permute-start.11 = (bf16[96,576]{1,0:T(8,128)(2,1)S(1)}, bf16[96,576]{1,0:T(8,128)(2,1)S(1)}, u32[]{:S(2)}, u32[]{:S(2)}) collective-permute-start(bf16[96,576]{1,0:T(8,128)(2,1)S(1)} %get-tuple-element.189), channel_id=1, source_target_pairs={{0,8},{8,16},{16,24},{24,0},{1,9},{9,17},{17,25},{25,1},{2,10},{10... | collective-permute-start | bytes 331784 | tf_op jit(solution)/shard_map/ppermute | solution.py:969
  348.7 21.2 %collective-permute-start.12 = (bf16[96,576]{1,0:T(8,128)(2,1)S(1)}, bf16[96,576]{1,0:T(8,128)(2,1)S(1)}, u32[]{:S(2)}, u32[]{:S(2)}) collective-permute-start(bf16[96,576]{1,0:T(8,128)(2,1)S(1)} %get-tuple-element.190), channel_id=1, source_target_pairs={{0,16},{8,24},{16,0},{24,8},{1,17},{9,25},{17,1},{25,9},{2,18},{10... | collective-permute-start | bytes 331784 | tf_op jit(solution)/shard_map/ppermute | solution.py:969
  351.1 18.8 %collective-permute-start.13 = (bf16[96,576]{1,0:T(8,128)(2,1)S(1)}, bf16[96,576]{1,0:T(8,128)(2,1)S(1)}, u32[]{:S(2)}, u32[]{:S(2)}) collective-permute-start(bf16[96,576]{1,0:T(8,128)(2,1)S(1)} %get-tuple-element.191), channel_id=1, source_target_pairs={{0,24},{8,0},{16,8},{24,16},{1,25},{9,1},{17,9},{25,17},{2,26},{10... | collective-permute-start | bytes 331784 | tf_op jit(solution)/shard_map/ppermute | solution.py:969
  (38 other events, 411.7 us)
Sparse Core Ops, SparseCore 0:
  10.1 22.3 all-gather.9
  36.8 44.5 all-gather.7
  82.9 69.0 all-gather.11
  157.8 29.8 all-gather.13

commit v2 on v1

--- a/solution.py
+++ b/solution.py
@@ -453,7 +453,8 @@
         dx = dfi_ref[:, cols] + nn(q_ref[...], wq_ref[:, cols]) + nn(kv_ref[...], wkv_ref[:, cols])
         dx_ref[:, cols] = dx.astype(BF)
 
-    columns(dx_ref.shape[1], back)
+    for n in range(0, dx_ref.shape[1], 256):
+        back(slice(n, n + 256))
 
 
 def project_back(full, half, w_all, d_first_in):

time: 387 us -> 385 us (level)
  no operation moved by 1% of the time
where the time goes in v2:
time: 385 us; the launch traced here: 384 us
  Pallas kernels  165 us (43%)
  starting transfers between devices  56.6 us (15%)
  blocking collectives  50.8 us (13%)
  local copies, waits for them, and re-layouts  33.3 us (9%)
  other arithmetic  32.7 us (8%)
  waiting for transfers between devices  30.8 us (8%)
  between operations  14.4 us (4%)
    pallas_call x2, Pallas kernels, attend_back(): pl.pallas_call(attend_back_body, grid=(steps,), in_specs=[col, col, line,...  43.6 us
    pallas_call x1, Pallas kernels, middle(): pl.pallas_call(functools.partial(middle_body, heads), grid_spec=pltpu.Pre...  42.8 us
    pallas_call x1, Pallas kernels, attend(): pl.pallas_call(attend_body, grid=(STEPS,), in_specs=[chunk(1), chunk(1),...  42.4 us
    all_to_all x1, blocking collectives, per_device(): x_own = lax.all_to_all(mine, 'sq', 0, 0, tiled=True).reshape(tokens, width)  26.5 us
    all_to_all x1, blocking collectives, per_device(): got = lax.all_to_all(done, PLANE, 0, 0, tiled=True)  24.3 us
    ppermute x13, starting transfers between devices, swap(): return lax.ppermute(x, axis, [(i, i ^ bit) for i in range(size)])  18.2 us
    ppermute x13, waiting for transfers between devices, swap(): return lax.ppermute(x, axis, [(i, i ^ bit) for i in range(size)])  17.7 us
    convert_element_type x9, other arithmetic, plus(): return (a.astype(F32) + b.astype(F32)).astype(BF)  17.1 us
  transfers between devices with their start and end apart: 32, of which 8 were waited for; matrix products, arithmetic and copies ran while one was open for 15% of the time, Pallas kernels for 43%

profile of v2, /device:TPU:0, one launch (start us, length us, event | category | flops | bytes accessed | tf_op | source)
XLA Modules:
  0.0 383.7 jit_solution(9407167490604259660)
XLA Ops:
  10.2 26.5 %all_to_all.40 = bf16[4,128,768]{2,1,0:T(8,128)(2,1)} all-to-all(bf16[4,128,768]{2,1,0:T(8,128)(2,1)S(1)} %constant_dynamic-slice_fusion.7), channel_id=1, replica_groups=mesh['sq'=4,'own'=2,'hx'=2,'hc'=2] {'sq'}, dimensions={0} | all-to-all | bytes 1572864 | tf_op jit(solution)/shard_map/all_to_all | solution.py:858
  40.1 2.9 pad_maximum_fusion
  46.9 3.5 all-to-all-start.1
  54.0 10.7 %prepare.1 = (s32[12,512,1]{2,1,0:T(8,128)}, s32[12,512,1]{2,1,0:T(8,128)}, s32[12,1,512]{2,1,0:T(1,128)}, s32[12,1,512]{2,1,0:T(1,128)}, f32[512,1]{1,0:T(8,128)}, /*index=5*/s32[12,1,512]{2,1,0:T(1,128)}) custom-call(s32[2]{0:T(128)} %pad_add_fusion.2.here_ref, s32[12,1,512]{2,1,0:T(1,128)} %reshape.398.q_ref, s32[12,1,512]{2,1,0:T(1,128)} %reshape.400.k_ref, ...), custom_call_target="tpu_custom_call" | custom-call | flops 1000000000 | bytes 1000000 | tf_op jit(solution)/shard_map/prepare/pallas_call | solution.py:126
  71.5 9.9 %all-gather.8.cloned.1.call-done.x_ref = bf16[4096,768]{1,0:T(8,128)(2,1)} async-done(((bf16[512,768]{1,0:T(8,128)(2,1)}), bf16[4096,768]{1,0:T(8,128)(2,1)}) %all-gather.8.cloned.1.call-update) | async-done | bytes 6291472 | tf_op jit(solution)/shard_map/all_gather | solution.py:863
  81.5 9.5 %project.1 = (bf16[2,1024,256]{2,1,0:T(8,128)(2,1)}, bf16[2,2048,256]{2,1,0:T(8,128)(2,1)}) custom-call(bf16[4096,768]{1,0:T(8,128)(2,1)} %all-gather.8.cloned.1.call-done.x_ref, bf16[768,384]{1,0:T(8,128)(2,1)} %concatenate.36.w_ref, f32[1,384]{1,0:T(1,128)} %broadcast_in_dim.100.b_ref), custom_call_target="tpu_custom_call" | custom-call | flops 1000000000 | bytes 1000000 | tf_op jit(solution)/shard_map/project/pallas_call | solution.py:164
  91.0 42.4 %attend.1 = (bf16[12,512,128]{2,1,0:T(8,128)(2,1)}, bf16[12,512,128]{2,1,0:T(8,128)(2,1)}, f32[12,512,1]{2,1,0:T(8,128)}, f32[12,8,128]{2,1,0:T(8,128)}, bf16[8,256,256]{2,1,0:T(8,128)(2,1)}) custom-call(s32[12,512,1]{2,1,0:T(8,128)} %get-tuple-element.118.pq_ref, s32[12,512,1]{2,1,0:T(8,128)} %get-tuple-element.119.pk_ref, ...), custom_call_target="tpu_custom_call" | custom-call | flops 1000000000 | bytes 1000000 | tf_op jit(solution)/shard_map/attend/pallas_call | solution.py:284
  133.3 24.3 %all_to_all.41.got_ref = bf16[8,256,256]{2,1,0:T(8,128)(2,1)} all-to-all(bf16[8,256,256]{2,1,0:T(8,128)(2,1)} %get-tuple-element.129), channel_id=1, replica_groups=mesh['sq'=4,'own'=2,'hx'=2,'hc'=2] {'own','hx','hc'}, dimensions={0} | all-to-all | bytes 2097152 | tf_op jit(solution)/shard_map/all_to_all | solution.py:937
  157.7 42.8 %middle.1 = (bf16[512,768]{1,0:T(8,128)(2,1)}, bf16[8,128,256]{2,1,0:T(8,128)(2,1)}, bf16[8,128,256]{2,1,0:T(8,128)(2,1)}, f32[512,768]{1,0:T(8,128)}, bf16[2,76...) custom-call(s32[1]{0:T(128)} %bitcast.26.hc_ref, ...), custom_call_target="tpu_custom_call" | custom-call | flops 1000000000 | bytes 1000000 | tf_op jit(solution)/shard_map/middle/pallas_call | solution.py:739
  201.9 4.2 %all-to-all-start.3 = ((bf16[8,128,256]{2,1,0:T(8,128)(2,1)}), bf16[8,128,256]{2,1,0:T(8,128)(2,1)}, u32[]{:S(2)}, u32[]{:S(2)}) async-start(bf16[8,128,256]{2,1,0:T(8,128)(2,1)} %get-tuple-element.136), calls=%async_computation.3 | async-start | bytes 1048576 | tf_op jit(solution)/shard_map/all_to_all | solution.py:983
  216.0 2.9 fusion.2
  222.4 3.5 all-to-all-start.4
  231.3 28.0 %attend_back.2.full_ref = bf16[8,384,256]{2,1,0:T(8,128)(2,1)} custom-call(s32[12,512,1]{2,1,0:T(8,128)} %get-tuple-element.118.pq_ref, s32[12,512,1]{2,1,0:T(8,128)} %get-tuple-element.119.pk_ref, s32[12,1,512]{2,1,0:T(1,128)} %get-tuple-element.120.pqr_ref, s32[12,1,512]{2,1,0:T(1,128)} %get-tuple-element.121.pkr_ref, bf16[1024,256]{1,0:T(8,128)(2,1)} %bitcast.42.td_ref, ...), custom_call_target="tpu_custom_call" | custom-call | flops 1000000000 | bytes 1000000 | tf_op jit(solution)/shard_map/attend_back/pallas_call | solution.py:358
  260.2 4.1 %all-to-all-start.5 = ((bf16[8,384,256]{2,1,0:T(8,128)(2,1)}), bf16[8,384,256]{2,1,0:T(8,128)(2,1)S(1)}, u32[]{:S(2)}, u32[]{:S(2)}) async-start(bf16[8,384,256]{2,1,0:T(8,128)(2,1)} %attend_back.2.full_ref), calls=%async_computation.5 | async-start | bytes 3145728 | tf_op jit(solution)/shard_map/all_to_all | solution.py:1019
  266.8 2.8 fusion.7
  276.5 15.6 %attend_back.3.half_ref = bf16[8,384,256]{2,1,0:T(8,128)(2,1)} custom-call(s32[12,512,1]{2,1,0:T(8,128)} %get-tuple-element.118.pq_ref, s32[12,512,1]{2,1,0:T(8,128)} %get-tuple-element.119.pk_ref, s32[12,1,512]{2,1,0:T(1,128)} %get-tuple-element.120.pqr_ref, s32[12,1,512]{2,1,0:T(1,128)} %get-tuple-element.121.pkr_ref, bf16[1024,256]{1,0:T(8,128)(2,1)} %bitcast.148, ...), custom_call_target="tpu_custom_call" | custom-call | flops 1000000000 | bytes 1000000 | tf_op jit(solution)/shard_map/attend_back/pallas_call | solution.py:358
  294.6 3.6 all-to-all-start.6
  307.1 9.9 %project_grad.1 = (bf16[768,384]{1,0:T(8,128)(2,1)}, f32[1,384]{1,0:T(1,128)}) custom-call(bf16[4096,768]{1,0:T(8,128)(2,1)} %all-gather.8.cloned.1.call-done.x_ref, bf16[8,384,256]{2,1,0:T(8,128)(2,1)} %attend_back.2.full_ref, bf16[8,384,256]{2,1,0:T(8,128)(2,1)} %attend_back.3.half_ref), custom_call_target="tpu_custom_call" | custom-call | flops 1000000000 | bytes 1000000 | tf_op jit(solution)/shard_map/project_grad/pallas_call | solution.py:417
  320.6 5.2 %collective-permute-done.10 = bf16[4,96,384]{2,1,0:T(8,128)(2,1)S(1)} collective-permute-done((bf16[4,96,384]{2,1,0:T(8,128)(2,1)S(1)}, bf16[4,96,384]{2,1,0:T(8,128)(2,1)S(1)}, u32[]{:S(2)}, u32[]{:S(2)}) %collective-permute-start.10) | collective-permute-done | bytes 294944 | tf_op jit(solution)/shard_map/ppermute | solution.py:808
  328.0 6.4 %project_back.1 = bf16[512,768]{1,0:T(8,128)(2,1)} custom-call(bf16[8,384,256]{2,1,0:T(8,128)(2,1)} %copy-done.2, bf16[8,384,256]{2,1,0:T(8,128)(2,1)} %copy-done.3, bf16[4,576,768]{2,1,0:T(8,128)(2,1)} %bitcast.142, f32[512,768]{1,0:T(8,128)} %get-tuple-element.183.dfi_ref), custom_call_target="tpu_custom_call" | custom-call | flops 1000000000 | bytes 1000000 | tf_op jit(solution)/shard_map/project_back/pallas_call | solution.py:463
  334.4 4.2 %all-to-all-start.7 = ((bf16[4,128,768]{2,1,0:T(8,128)(2,1)}), bf16[4,128,768]{2,1,0:T(8,128)(2,1)}, u32[]{:S(2)}, u32[]{:S(2)}) async-start(bf16[4,128,768]{2,1,0:T(8,128)(2,1)} %bitcast.144), calls=%async_computation.7 | async-start | bytes 1572864 | tf_op jit(solution)/shard_map/all_to_all | solution.py:1065
  352.8 8.3 %collective-permute-done.17 = f32[9216]{0:T(1024)S(1)} collective-permute-done((f32[9216]{0:T(1024)S(1)}, f32[9216]{0:T(1024)S(1)}, u32[]{:S(2)}, u32[]{:S(2)}) %collective-permute-start.17) | collective-permute-done | bytes 36896 | tf_op jit(solution)/shard_map/ppermute | solution.py:808
  361.1 4.5 %collective-permute-start.18 = (f32[9216]{0:T(1024)S(1)}, f32[9216]{0:T(1024)S(1)}, u32[]{:S(2)}, u32[]{:S(2)}) collective-permute-start(f32[9216]{0:T(1024)S(1)} %add.263), channel_id=1, source_target_pairs={{0,16},{8,24},{16,0},{24,8},{1,17},{9,25},{17,1},{25,9},{2,18},{10... | collective-permute-start | bytes 110600 | tf_op jit(solution)/shard_map/ppermute | solution.py:808
  365.6 3.1 collective-permute-done.12
  (210 shorter events, 90.6 us)
Async XLA Ops:
  7.2 29.5 %all-gather.10.cloned.1.call-start = ((), (), s32[]{:S(2)}) async-start(), calls=%async_computation.9 | async-start | bytes 1966080 | tf_op jit(solution)/shard_map/all_gather | solution.py:859
  10.0 71.4 %all-gather.8.cloned.1.call-start = ((), (), s32[]{:S(2)}) async-start(), calls=%async_computation.8 | async-start | bytes 7077888 | tf_op jit(solution)/shard_map/all_gather | solution.py:863
  46.9 24.6 %all-to-all-start.1 = ((bf16[4,128,768]{2,1,0:T(8,128)(2,1)}), bf16[4,128,768]{2,1,0:T(8,128)(2,1)S(1)}, u32[]{:S(2)}, u32[]{:S(2)}) async-start(bf16[4,128,768]{2,1,0:T(8,128)(2,1)} %param.24), calls=%async_computation.1 | async-start | bytes 1572864 | tf_op jit(solution)/shard_map/all_to_all | solution.py:864
  50.4 107.2 %all-gather.12.cloned.1.call-start = ((), (), s32[]{:S(2)}) async-start(), calls=%async_computation.10 | async-start | bytes 11796480 | tf_op jit(solution)/shard_map/all_gather | solution.py:933
  81.4 137.5 %all-gather.14.cloned.1.call-start = ((), (), s32[]{:S(2)}) async-start(), calls=%async_computation.11 | async-start | bytes 4423680 | tf_op jit(solution)/shard_map/all_gather | solution.py:941
  201.3 17.6 %collective-permute-start = (f32[16]{0:T(128)S(1)}, f32[16]{0:T(128)S(1)}, u32[]{:S(2)}, u32[]{:S(2)}) collective-permute-start(f32[16]{0:T(128)S(1)} %broadcast_select_fusion.3), channel_id=1, source_target_pairs={{0,4},{4,0},{1,5},{5,1},{2,6},{6,2},{3,7},{7,3},{8,12},{12,8},{9,1... | collective-permute-start | bytes 200 | tf_op jit(solution)/shard_map/ppermute | solution.py:808
  201.9 17.0 %all-to-all-start.3 = ((bf16[8,128,256]{2,1,0:T(8,128)(2,1)}), bf16[8,128,256]{2,1,0:T(8,128)(2,1)}, u32[]{:S(2)}, u32[]{:S(2)}) async-start(bf16[8,128,256]{2,1,0:T(8,128)(2,1)} %get-tuple-element.136), calls=%async_computation.3 | async-start | bytes 1048576 | tf_op jit(solution)/shard_map/all_to_all | solution.py:983
  218.9 40.4 %collective-permute-start.3 = (bf16[4,2,96,896]{3,2,0,1:T(8,128)(2,1)}, bf16[4,2,96,896]{3,2,0,1:T(8,128)(2,1)}, u32[]{:S(2)}, u32[]{:S(2)}) collective-permute-start(bf16[4,2,96,896]{3,2,0,1:T(8,128)(2,1)} %fusion), channel_id=1, source_target_pairs={{0,2},{2,0},{1,3},{3,1},{4,6},{6,4},{5,7},{7,5},{8,10},{10,8},{9,1... | collective-permute-start | bytes 4128776 | tf_op jit(solution)/shard_map/ppermute | solution.py:808
  220.9 38.5 %collective-permute-start.4 = (bf16[2,4,96,896]{3,2,1,0:T(8,128)(2,1)}, bf16[2,4,96,896]{3,2,1,0:T(8,128)(2,1)}, u32[]{:S(2)}, u32[]{:S(2)}) collective-permute-start(bf16[2,4,96,896]{3,2,1,0:T(8,128)(2,1)} %fusion.2), channel_id=1, source_target_pairs={{0,4},{4,0},{1,5},{5,1},{2,6},{6,2},{3,7},{7,3},{8,12},{12,8},{9,1... | collective-permute-start | bytes 4128776 | tf_op jit(solution)/shard_map/ppermute | solution.py:808
  222.4 36.9 %all-to-all-start.4 = ((bf16[8,128,256]{2,1,0:T(8,128)(2,1)}), bf16[8,128,256]{2,1,0:T(8,128)(2,1)S(1)}, u32[]{:S(2)}, u32[]{:S(2)}) async-start(bf16[8,128,256]{2,1,0:T(8,128)(2,1)} %get-tuple-element.149), calls=%async_computation.4 | async-start | bytes 1048576 | tf_op jit(solution)/shard_map/all_to_all | solution.py:1012
  225.9 33.4 %collective-permute-start.5 = (bf16[128,768]{1,0:T(8,128)(2,1)S(1)}, bf16[128,768]{1,0:T(8,128)(2,1)S(1)}, u32[]{:S(2)}, u32[]{:S(2)}) collective-permute-start(bf16[128,768]{1,0:T(8,128)(2,1)S(1)} %copy-done.20), channel_id=1, source_target_pairs={{0,8},{8,16},{16,24},{24,0},{1,9},{9,17},{17,25},{25,1},{2,10},{10... | collective-permute-start | bytes 589832 | tf_op jit(solution)/shard_map/ppermute | solution.py:970
  227.4 31.8 %collective-permute-start.6 = (bf16[128,768]{1,0:T(8,128)(2,1)S(1)}, bf16[128,768]{1,0:T(8,128)(2,1)S(1)}, u32[]{:S(2)}, u32[]{:S(2)}) collective-permute-start(bf16[128,768]{1,0:T(8,128)(2,1)S(1)} %get-tuple-element.154), channel_id=1, source_target_pairs={{0,16},{8,24},{16,0},{24,8},{1,17},{9,25},{17,1},{25,9},{2,18},{10... | collective-permute-start | bytes 589832 | tf_op jit(solution)/shard_map/ppermute | solution.py:970
  229.8 29.5 %collective-permute-start.7 = (bf16[128,768]{1,0:T(8,128)(2,1)S(1)}, bf16[128,768]{1,0:T(8,128)(2,1)S(1)}, u32[]{:S(2)}, u32[]{:S(2)}) collective-permute-start(bf16[128,768]{1,0:T(8,128)(2,1)S(1)} %get-tuple-element.155), channel_id=1, source_target_pairs={{0,24},{8,0},{16,8},{24,16},{1,25},{9,1},{17,9},{25,17},{2,26},{10... | collective-permute-start | bytes 589832 | tf_op jit(solution)/shard_map/ppermute | solution.py:970
  260.2 33.3 %all-to-all-start.5 = ((bf16[8,384,256]{2,1,0:T(8,128)(2,1)}), bf16[8,384,256]{2,1,0:T(8,128)(2,1)S(1)}, u32[]{:S(2)}, u32[]{:S(2)}) async-start(bf16[8,384,256]{2,1,0:T(8,128)(2,1)} %attend_back.2.full_ref), calls=%async_computation.5 | async-start | bytes 3145728 | tf_op jit(solution)/shard_map/all_to_all | solution.py:1019
  272.4 26.8 %collective-permute-start.8 = (bf16[4,96,896]{2,1,0:T(8,128)(2,1)}, bf16[4,96,896]{2,1,0:T(8,128)(2,1)}, u32[]{:S(2)}, u32[]{:S(2)}) collective-permute-start(bf16[4,96,896]{2,1,0:T(8,128)(2,1)} %get-tuple-element.169), channel_id=1, source_target_pairs={{0,4},{4,0},{1,5},{5,1},{2,6},{6,2},{3,7},{7,3},{8,12},{12,8},{9,1... | collective-permute-start | bytes 2064392 | tf_op jit(solution)/shard_map/ppermute | solution.py:808
  274.4 24.9 %collective-permute-start.9 = (bf16[4,96,896]{2,1,0:T(8,128)(2,1)}, bf16[4,96,896]{2,1,0:T(8,128)(2,1)}, u32[]{:S(2)}, u32[]{:S(2)}) collective-permute-start(bf16[4,96,896]{2,1,0:T(8,128)(2,1)} %get-tuple-element.170), channel_id=1, source_target_pairs={{0,2},{2,0},{1,3},{3,1},{4,6},{6,4},{5,7},{7,5},{8,10},{10,8},{9,1... | collective-permute-start | bytes 2064392 | tf_op jit(solution)/shard_map/ppermute | solution.py:808
  294.6 31.2 %all-to-all-start.6 = ((bf16[8,384,256]{2,1,0:T(8,128)(2,1)}), bf16[8,384,256]{2,1,0:T(8,128)(2,1)S(1)}, u32[]{:S(2)}, u32[]{:S(2)}) async-start(bf16[8,384,256]{2,1,0:T(8,128)(2,1)} %attend_back.3.half_ref), calls=%async_computation.6 | async-start | bytes 3145728 | tf_op jit(solution)/shard_map/all_to_all | solution.py:1030
  303.0 35.5 %collective-permute-start.19 = (bf16[96,1792]{1,0:T(8,128)(2,1)}, bf16[96,1792]{1,0:T(8,128)(2,1)}, u32[]{:S(2)}, u32[]{:S(2)}) collective-permute-start(bf16[96,1792]{1,0:T(8,128)(2,1)} %get-tuple-element.194), channel_id=1, source_target_pairs={{0,8},{8,16},{16,24},{24,0},{1,9},{9,17},{17,25},{25,1},{2,10},{10... | collective-permute-start | bytes 1032200 | tf_op jit(solution)/shard_map/ppermute | solution.py:970
  303.7 34.9 %collective-permute-start.20 = (bf16[96,1792]{1,0:T(8,128)(2,1)}, bf16[96,1792]{1,0:T(8,128)(2,1)}, u32[]{:S(2)}, u32[]{:S(2)}) collective-permute-start(bf16[96,1792]{1,0:T(8,128)(2,1)} %get-tuple-element.195), channel_id=1, source_target_pairs={{0,16},{8,24},{16,0},{24,8},{1,17},{9,25},{17,1},{25,9},{2,18},{10... | collective-permute-start | bytes 1032200 | tf_op jit(solution)/shard_map/ppermute | solution.py:970
  305.6 33.0 %collective-permute-start.21 = (bf16[96,1792]{1,0:T(8,128)(2,1)}, bf16[96,1792]{1,0:T(8,128)(2,1)}, u32[]{:S(2)}, u32[]{:S(2)}) collective-permute-start(bf16[96,1792]{1,0:T(8,128)(2,1)} %get-tuple-element.196), channel_id=1, source_target_pairs={{0,24},{8,0},{16,8},{24,16},{1,25},{9,1},{17,9},{25,17},{2,26},{10... | collective-permute-start | bytes 1032200 | tf_op jit(solution)/shard_map/ppermute | solution.py:970
  334.4 40.4 %all-to-all-start.7 = ((bf16[4,128,768]{2,1,0:T(8,128)(2,1)}), bf16[4,128,768]{2,1,0:T(8,128)(2,1)}, u32[]{:S(2)}, u32[]{:S(2)}) async-start(bf16[4,128,768]{2,1,0:T(8,128)(2,1)} %bitcast.144), calls=%async_computation.7 | async-start | bytes 1572864 | tf_op jit(solution)/shard_map/all_to_all | solution.py:1065
  345.6 20.1 %collective-permute-start.11 = (bf16[96,576]{1,0:T(8,128)(2,1)S(1)}, bf16[96,576]{1,0:T(8,128)(2,1)S(1)}, u32[]{:S(2)}, u32[]{:S(2)}) collective-permute-start(bf16[96,576]{1,0:T(8,128)(2,1)S(1)} %get-tuple-element.189), channel_id=1, source_target_pairs={{0,8},{8,16},{16,24},{24,0},{1,9},{9,17},{17,25},{25,1},{2,10},{10... | collective-permute-start | bytes 331784 | tf_op jit(solution)/shard_map/ppermute | solution.py:970
  347.6 21.2 %collective-permute-start.12 = (bf16[96,576]{1,0:T(8,128)(2,1)S(1)}, bf16[96,576]{1,0:T(8,128)(2,1)S(1)}, u32[]{:S(2)}, u32[]{:S(2)}) collective-permute-start(bf16[96,576]{1,0:T(8,128)(2,1)S(1)} %get-tuple-element.190), channel_id=1, source_target_pairs={{0,16},{8,24},{16,0},{24,8},{1,17},{9,25},{17,1},{25,9},{2,18},{10... | collective-permute-start | bytes 331784 | tf_op jit(solution)/shard_map/ppermute | solution.py:970
  349.9 18.8 %collective-permute-start.13 = (bf16[96,576]{1,0:T(8,128)(2,1)S(1)}, bf16[96,576]{1,0:T(8,128)(2,1)S(1)}, u32[]{:S(2)}, u32[]{:S(2)}) collective-permute-start(bf16[96,576]{1,0:T(8,128)(2,1)S(1)} %get-tuple-element.191), channel_id=1, source_target_pairs={{0,24},{8,0},{16,8},{24,16},{1,25},{9,1},{17,9},{25,17},{2,26},{10... | collective-permute-start | bytes 331784 | tf_op jit(solution)/shard_map/ppermute | solution.py:970
  (38 other events, 411.7 us)
Sparse Core Ops, SparseCore 0:
  10.1 22.3 all-gather.9
  36.8 44.5 all-gather.7
  82.9 69.0 all-gather.11
  157.8 29.8 all-gather.13
